TPU v7x, 32 devices: a whole 2x2x4 slice. The times are simulated.
32 devices in a mesh: rows: 4 (over x, core), cols: 8 (over z, y).
Axes of the slice: x: 2, y: 2, z: 4, core: 2. Of those that a mesh axis runs over, the one named last changes fastest.
Arguments:
- image: bfloat16 [48, 64, 2048], P(None, 'rows', 'cols'), may hold values from -6 to 6
- perturb: float32 [48, 64, 2048], P(None, 'rows', 'cols'), may hold values from -0.5 to 0.5
- target: bfloat16 [48, 32, 1024], P(None, 'rows', 'cols'), may hold values from -6 to 6
- kernel_one: float32 [48, 48, 3, 3], replicated, may hold values from -0.3125 to 0.3125
- kernel_two: float32 [48, 48, 3, 3], replicated, may hold values from -0.3125 to 0.3125
- moment_one: float32 [48, 48, 3, 3], replicated, may hold values from -6 to 6
- moment_two: float32 [48, 48, 3, 3], replicated, may hold values from -6 to 6
Outputs:
- new_perturb: float32 [48, 64, 2048], P(None, 'rows', 'cols')
- prediction: bfloat16 [48, 32, 1024], P(None, 'rows', 'cols')
- new_kernel_one: float32 [48, 48, 3, 3], replicated
- new_kernel_two: float32 [48, 48, 3, 3], replicated
- new_moment_one: float32 [48, 48, 3, 3], replicated
- new_moment_two: float32 [48, 48, 3, 3], replicated
All inputs are finite; a program needn't handle non-finite values.
Results may differ from a plain program's by a relative error of at most 0.0085.
Values may be sent and summed in bfloat16 or wider, within the bound.
A program may use at most 128 MiB of HBM per device.

v0:
```python
import jax
import jax.numpy as jnp
from jax import lax
from jax.sharding import PartitionSpec as P

REPLAYS = 3


step_size = 0.5
clip_bound = 0.5
momentum_rate = 0.9
learn_rate = 0.005
mean_epsilon = 1e-06
numbers = ("NCHW", "OIHW", "NCHW")


def with_halo(block, sides, width):
    for axis, dim in sides:
        count = lax.axis_size(axis)
        forward = [(i, i + 1) for i in range(count - 1)]
        backward = [(target, source) for source, target in forward]
        low = lax.ppermute(
            lax.slice_in_dim(block, block.shape[dim] - width, None, axis=dim), axis, forward
        )
        high = lax.ppermute(lax.slice_in_dim(block, 0, width, axis=dim), axis, backward)
        block = jnp.concatenate([low, block, high], axis=dim)
    return block


def shifted(block, axis, distance):
    devices = range(lax.axis_size(axis))
    route = [(i - distance, i) for i in devices if i - distance in devices]
    return lax.ppermute(block, axis, route)


def plain_conv(source, kernel, stride, dilation):
    return lax.conv_general_dilated(
        source[None],
        kernel,
        (stride, stride),
        "VALID",
        rhs_dilation=(dilation, dilation),
        dimension_numbers=numbers,
        preferred_element_type=jnp.float32,
    )[0]


def kernel_grad(source, grad_out, stride, dilation):
    summed = lax.conv_general_dilated(
        source[None],
        grad_out[None],
        (dilation, dilation),
        "VALID",
        rhs_dilation=(stride, stride),
        dimension_numbers=("CNHW", "IOHW", "NCHW"),
        preferred_element_type=jnp.float32,
    )
    return jnp.transpose(summed, (1, 0, 2, 3))


def flipped(kernel):
    return jnp.transpose(kernel, (1, 0, 2, 3))[:, :, ::-1, ::-1]


def spread_grad(grad_out, kernel):
    return lax.conv_general_dilated(
        grad_out[None],
        flipped(kernel),
        (1, 1),
        ((2, 2), (2, 2)),
        lhs_dilation=(2, 2),
        dimension_numbers=numbers,
        preferred_element_type=jnp.float32,
    )[0]


def silu_slope(pre_value):
    sigmoid_value = jax.nn.sigmoid(pre_value)
    return sigmoid_value * (1.0 + pre_value * (1.0 - sigmoid_value))


def normed_update(kernel, moment, gradient, mean_square):
    moment = momentum_rate * moment + gradient / jnp.sqrt(mean_square + mean_epsilon)
    return (kernel - learn_rate * moment, moment)


def body(image, perturb, target, kernel_one, kernel_two, moment_one, moment_two):
    target_wide = target.astype(jnp.float32)
    learned = [kernel_one, moment_one, kernel_two, moment_two]
    fast_one = kernel_one.astype(jnp.bfloat16)
    fast_two = kernel_two.astype(jnp.bfloat16)
    predict = jnp.zeros(target.shape, jnp.float32)
    for replay in range(REPLAYS):
        attacked = (image.astype(jnp.float32) + perturb).astype(jnp.bfloat16)
        beside_all = with_halo(attacked, (("rows", 1), ("cols", 2)), 2)
        hidden_pre = plain_conv(beside_all, fast_one, 1, 2)
        hidden = jax.nn.silu(hidden_pre).astype(jnp.bfloat16)
        left_col = shifted(hidden[:, :, -1:], "cols", 1)
        widened = jnp.concatenate([left_col, hidden], axis=2)
        top_row = shifted(widened[:, -1:, :], "rows", 1)
        extended = jnp.concatenate([top_row, widened], axis=1)
        predict = plain_conv(extended, fast_two, 2, 1)
        residual = (predict - target_wide).astype(jnp.bfloat16)
        grad_two = kernel_grad(extended, residual, 2, 1)
        grad_two = lax.psum(grad_two, ("rows", "cols"))
        spread = spread_grad(residual, fast_two)
        from_below = shifted(spread[:, :1, :].astype(jnp.bfloat16), "rows", -1).astype(jnp.float32)
        widened_grad = spread[:, 1:, :].at[:, -1:, :].add(from_below)
        from_right = shifted(widened_grad[:, :, :1], "cols", -1)
        hidden_grad = widened_grad[:, :, 1:].at[:, :, -1:].add(from_right)
        pre_grad = (hidden_grad * silu_slope(hidden_pre)).astype(jnp.bfloat16)
        grad_rimmed = with_halo(pre_grad, (("rows", 1), ("cols", 2)), 2)
        input_grad = plain_conv(grad_rimmed, flipped(fast_one), 1, 2)
        grad_one = kernel_grad(beside_all, pre_grad, 1, 2)
        perturb = jnp.clip(perturb + step_size * jnp.tanh(input_grad), -clip_bound, clip_bound)
        grad_one = lax.psum(grad_one, ("rows", "cols"))
        new_one, new_moment_one = normed_update(
            learned[0], learned[1], grad_one, jnp.mean(grad_one * grad_one)
        )
        new_two, new_moment_two = normed_update(
            learned[2], learned[3], grad_two, jnp.mean(grad_two * grad_two)
        )
        learned = [new_one, new_moment_one, new_two, new_moment_two]
        fast_one = new_one.astype(jnp.bfloat16)
        fast_two = new_two.astype(jnp.bfloat16)
    return (perturb, predict.astype(jnp.bfloat16), learned[0], learned[2], learned[1], learned[3])


def solution(mesh):
    in_specs = (
        P(None, "rows", "cols"),
        P(None, "rows", "cols"),
        P(None, "rows", "cols"),
        P(),
        P(),
        P(),
        P(),
    )
    out_specs = (P(None, "rows", "cols"), P(None, "rows", "cols"), P(), P(), P(), P())
    return jax.shard_map(body, mesh=mesh, in_specs=in_specs, out_specs=out_specs, check_vma=False)
```

profile of v0, /device:TPU:0, one launch (start us, length us, event | category | flops | bytes accessed | tf_op | source)
XLA Modules:
  0.0 782.1 jit_solution(5333286303783374361)
XLA Ops:
  49.2 5.3 collective-permute-start.5
  79.4 5.1 scatter-add.20
  91.7 4.9 copy.320
  104.8 5.5 collective-permute-start.8
  111.6 5.5 fusion.109
  118.3 5.0 collective-permute-start.10
  125.0 14.8 %fusion.22 = f32[48,48,3,3]{0,1,3,2:T(8,128)} fusion(bf16[1,48,20,260]{1,0,3,2:T(2,128)(2,1)} %copy.320, bf16[1,48,16,256]{1,2,3,0:T(8,128)(2,1)S(1)} %bitcast.267), kind=kOutput, calls=%fused_computation.48 | convolution fusion | flops 169869312 | bytes 975360 | tf_op jit(solution)/shard_map/transpose | solution.py:58
  156.2 115.3 %all-reduce.11.cloned.1.call-done = (f32[48,48,3,3]{0,1,3,2:T(8,128)}, f32[48,48,3,3]{0,1,3,2:T(8,128)}) async-done(((f32[48,48,3,3]{0,1,3,2:T(8,128)}, f32[48,48,3,3]{0,1,3,2:T(8,128)}), (f32[48,48,3,3]{0,1,3,2:T(8,128)}, f32[48,48,3,3]{0,1,3,2:T(8,128)})) %all-reduce.11.cloned.1.call-update) | async-done | bytes 165904 | tf_op jit(solution)/shard_map/psum | solution.py:116
  280.5 8.1 %collective-permute-done.14 = bf16[48,20,2]{2,0,1:T(8,128)(2,1)S(1)} collective-permute-done((bf16[48,20,2]{2,0,1:T(8,128)(2,1)S(1)}, bf16[48,20,2]{2,0,1:T(8,128)(2,1)S(1)}, u32[]{:S(2)}, u32[]{:S(2)}) %collective-permute-start.14) | collective-permute-done | bytes 3872 | tf_op jit(solution)/shard_map/ppermute | solution.py:22
  298.4 4.8 collective-permute-start.16
  328.4 5.1 scatter-add.24
  335.4 4.9 copy.348
  348.5 6.2 collective-permute-start.20
  356.0 5.5 fusion.107
  362.8 5.4 collective-permute-start.22
  369.6 14.8 %fusion.20 = f32[48,48,3,3]{0,1,3,2:T(8,128)} fusion(bf16[1,48,20,260]{1,0,3,2:T(2,128)(2,1)} %copy.348, bf16[1,48,16,256]{1,2,3,0:T(8,128)(2,1)S(1)} %bitcast.268), kind=kOutput, calls=%fused_computation.46 | convolution fusion | flops 169869312 | bytes 975360 | tf_op jit(solution)/shard_map/transpose | solution.py:58
  401.5 113.6 %all-reduce.9.cloned.1.call-done = (f32[48,48,3,3]{0,1,3,2:T(8,128)}, f32[48,48,3,3]{0,1,3,2:T(8,128)}) async-done(((f32[48,48,3,3]{0,1,3,2:T(8,128)}, f32[48,48,3,3]{0,1,3,2:T(8,128)}), (f32[48,48,3,3]{0,1,3,2:T(8,128)}, f32[48,48,3,3]{0,1,3,2:T(8,128)})) %all-reduce.9.cloned.1.call-update) | async-done | bytes 165904 | tf_op jit(solution)/shard_map/psum | solution.py:116
  525.0 8.2 %collective-permute-done.26 = bf16[48,20,2]{2,0,1:T(8,128)(2,1)S(1)} collective-permute-done((bf16[48,20,2]{2,0,1:T(8,128)(2,1)S(1)}, bf16[48,20,2]{2,0,1:T(8,128)(2,1)S(1)}, u32[]{:S(2)}, u32[]{:S(2)}) %collective-permute-start.26) | collective-permute-done | bytes 3872 | tf_op jit(solution)/shard_map/ppermute | solution.py:22
  573.8 4.9 copy.368
  588.2 5.1 scatter-add.26
  595.3 7.1 fusion.105
  613.1 5.4 collective-permute-start.34
  620.0 14.8 %fusion.18 = f32[48,48,3,3]{0,1,3,2:T(8,128)} fusion(bf16[1,48,20,260]{1,0,3,2:T(2,128)(2,1)} %copy.368, bf16[1,48,16,256]{1,2,3,0:T(8,128)(2,1)S(1)} %bitcast.269), kind=kOutput, calls=%fused_computation.44 | convolution fusion | flops 169869312 | bytes 975360 | tf_op jit(solution)/shard_map/transpose | solution.py:58
  648.0 119.0 %all-reduce.7.cloned.1.call-done = (f32[48,48,3,3]{0,1,3,2:T(8,128)}, f32[48,48,3,3]{0,1,3,2:T(8,128)}) async-done(((f32[48,48,3,3]{0,1,3,2:T(8,128)}, f32[48,48,3,3]{0,1,3,2:T(8,128)}), (f32[48,48,3,3]{0,1,3,2:T(8,128)}, f32[48,48,3,3]{0,1,3,2:T(8,128)})) %all-reduce.7.cloned.1.call-update) | async-done | bytes 165904 | tf_op jit(solution)/shard_map/psum | solution.py:116
  (396 shorter events, 267.6 us)
Async XLA Ops:
  7.2 264.3 %all-reduce.11.cloned.1.call-start = ((), (), s32[]{:S(2)}) async-start(), calls=%async_computation.2 | async-start | bytes 884736 | tf_op jit(solution)/shard_map/psum | solution.py:116
  49.2 8.9 %collective-permute-start.5 = (bf16[48,1,257]{0,1,2:T(2,128)(2,1)}, bf16[48,1,257]{0,1,2:T(2,128)(2,1)}, u32[]{:S(2)}, u32[]{:S(2)}) collective-permute-start(bf16[48,1,257]{0,1,2:T(2,128)(2,1)} %fusion.141), channel_id=1, source_target_pairs={{0,8},{8,16},{16,24},{1,9},{9,17},{17,25},{2,10},{10,18},{18,26},{... | collective-permute-start | bytes 74024 | tf_op jit(solution)/shard_map/ppermute | solution.py:33
  85.2 17.8 %collective-permute-start.7 = (f32[48,16,1]{0,1,2:T(8,128)S(1)}, f32[48,16,1]{0,1,2:T(8,128)S(1)}, u32[]{:S(2)}, u32[]{:S(2)}) collective-permute-start(f32[48,16,1]{0,1,2:T(8,128)S(1)} %slice.369), channel_id=1, source_target_pairs={{1,0},{2,1},{3,2},{4,3},{5,4},{6,5},{7,6},{9,8},{10,9},{11,10},{12... | collective-permute-start | bytes 9224 | tf_op jit(solution)/shard_map/ppermute | solution.py:33
  104.8 13.2 %collective-permute-start.8 = (bf16[48,2,256]{0,1,2:T(2,128)(2,1)S(1)}, bf16[48,2,256]{0,1,2:T(2,128)(2,1)S(1)}, u32[]{:S(2)}, u32[]{:S(2)}) collective-permute-start(bf16[48,2,256]{0,1,2:T(2,128)(2,1)S(1)} %get-tuple-element.130), channel_id=1, source_target_pairs={{0,8},{8,16},{16,24},{1,9},{9,17},{17,25},{2,10},{10,18},{18,26},{... | collective-permute-start | bytes 147464 | tf_op jit(solution)/shard_map/ppermute | solution.py:22
  118.3 21.7 %collective-permute-start.10 = (bf16[48,20,2]{2,0,1:T(8,128)(2,1)S(1)}, bf16[48,20,2]{2,0,1:T(8,128)(2,1)S(1)}, u32[]{:S(2)}, u32[]{:S(2)}) collective-permute-start(bf16[48,20,2]{2,0,1:T(8,128)(2,1)S(1)} %get-tuple-element.160), channel_id=1, source_target_pairs={{0,1},{1,2},{2,3},{3,4},{4,5},{5,6},{6,7},{8,9},{9,10},{10,11},{11... | collective-permute-start | bytes 11528 | tf_op jit(solution)/shard_map/ppermute | solution.py:22
  123.3 16.7 %collective-permute-start.11 = (bf16[48,20,2]{2,0,1:T(8,128)(2,1)S(1)}, bf16[48,20,2]{2,0,1:T(8,128)(2,1)S(1)}, u32[]{:S(2)}, u32[]{:S(2)}) collective-permute-start(bf16[48,20,2]{2,0,1:T(8,128)(2,1)S(1)} %get-tuple-element.161), channel_id=1, source_target_pairs={{1,0},{2,1},{3,2},{4,3},{5,4},{6,5},{7,6},{9,8},{10,9},{11,10},{12... | collective-permute-start | bytes 11528 | tf_op jit(solution)/shard_map/ppermute | solution.py:25
  139.8 375.3 %all-reduce.9.cloned.1.call-start = ((), (), s32[]{:S(2)}) async-start(), calls=%async_computation.1 | async-start | bytes 884736 | tf_op jit(solution)/shard_map/psum | solution.py:116
  152.1 121.8 %collective-permute-start.12 = (bf16[48,2,256]{0,1,2:T(2,128)(2,1)S(1)}, bf16[48,2,256]{0,1,2:T(2,128)(2,1)S(1)}, u32[]{:S(2)}, u32[]{:S(2)}) collective-permute-start(bf16[48,2,256]{0,1,2:T(2,128)(2,1)S(1)} %get-tuple-element.128), channel_id=1, source_target_pairs={{0,8},{8,16},{16,24},{1,9},{9,17},{17,25},{2,10},{10,18},{18,26},{... | collective-permute-start | bytes 147464 | tf_op jit(solution)/shard_map/ppermute | solution.py:22
  154.9 119.1 %collective-permute-start.13 = (bf16[48,2,256]{0,1,2:T(2,128)(2,1)S(1)}, bf16[48,2,256]{0,1,2:T(2,128)(2,1)S(1)}, u32[]{:S(2)}, u32[]{:S(2)}) collective-permute-start(bf16[48,2,256]{0,1,2:T(2,128)(2,1)S(1)} %get-tuple-element.129), channel_id=1, source_target_pairs={{8,0},{16,8},{24,16},{9,1},{17,9},{25,17},{10,2},{18,10},{26,18},{... | collective-permute-start | bytes 147464 | tf_op jit(solution)/shard_map/ppermute | solution.py:25
  274.3 14.3 %collective-permute-start.14 = (bf16[48,20,2]{2,0,1:T(8,128)(2,1)S(1)}, bf16[48,20,2]{2,0,1:T(8,128)(2,1)S(1)}, u32[]{:S(2)}, u32[]{:S(2)}) collective-permute-start(bf16[48,20,2]{2,0,1:T(8,128)(2,1)S(1)} %get-tuple-element.158), channel_id=1, source_target_pairs={{0,1},{1,2},{2,3},{3,4},{4,5},{5,6},{6,7},{8,9},{9,10},{10,11},{11... | collective-permute-start | bytes 11528 | tf_op jit(solution)/shard_map/ppermute | solution.py:22
  277.7 10.9 %collective-permute-start.15 = (bf16[48,20,2]{2,0,1:T(8,128)(2,1)S(1)}, bf16[48,20,2]{2,0,1:T(8,128)(2,1)S(1)}, u32[]{:S(2)}, u32[]{:S(2)}) collective-permute-start(bf16[48,20,2]{2,0,1:T(8,128)(2,1)S(1)} %get-tuple-element.159), channel_id=1, source_target_pairs={{1,0},{2,1},{3,2},{4,3},{5,4},{6,5},{7,6},{9,8},{10,9},{11,10},{12... | collective-permute-start | bytes 11528 | tf_op jit(solution)/shard_map/ppermute | solution.py:25
  334.1 12.6 %collective-permute-start.19 = (f32[48,16,1]{0,1,2:T(8,128)S(1)}, f32[48,16,1]{0,1,2:T(8,128)S(1)}, u32[]{:S(2)}, u32[]{:S(2)}) collective-permute-start(f32[48,16,1]{0,1,2:T(8,128)S(1)} %slice.394), channel_id=1, source_target_pairs={{1,0},{2,1},{3,2},{4,3},{5,4},{6,5},{7,6},{9,8},{10,9},{11,10},{12... | collective-permute-start | bytes 9224 | tf_op jit(solution)/shard_map/ppermute | solution.py:33
  348.5 13.9 %collective-permute-start.20 = (bf16[48,2,256]{0,1,2:T(2,128)(2,1)S(1)}, bf16[48,2,256]{0,1,2:T(2,128)(2,1)S(1)}, u32[]{:S(2)}, u32[]{:S(2)}) collective-permute-start(bf16[48,2,256]{0,1,2:T(2,128)(2,1)S(1)} %get-tuple-element.126), channel_id=1, source_target_pairs={{0,8},{8,16},{16,24},{1,9},{9,17},{17,25},{2,10},{10,18},{18,26},{... | collective-permute-start | bytes 147464 | tf_op jit(solution)/shard_map/ppermute | solution.py:22
  362.8 22.1 %collective-permute-start.22 = (bf16[48,20,2]{2,0,1:T(8,128)(2,1)S(1)}, bf16[48,20,2]{2,0,1:T(8,128)(2,1)S(1)}, u32[]{:S(2)}, u32[]{:S(2)}) collective-permute-start(bf16[48,20,2]{2,0,1:T(8,128)(2,1)S(1)} %get-tuple-element.156), channel_id=1, source_target_pairs={{0,1},{1,2},{2,3},{3,4},{4,5},{5,6},{6,7},{8,9},{9,10},{10,11},{11... | collective-permute-start | bytes 11528 | tf_op jit(solution)/shard_map/ppermute | solution.py:22
  368.1 16.7 %collective-permute-start.23 = (bf16[48,20,2]{2,0,1:T(8,128)(2,1)S(1)}, bf16[48,20,2]{2,0,1:T(8,128)(2,1)S(1)}, u32[]{:S(2)}, u32[]{:S(2)}) collective-permute-start(bf16[48,20,2]{2,0,1:T(8,128)(2,1)S(1)} %get-tuple-element.157), channel_id=1, source_target_pairs={{1,0},{2,1},{3,2},{4,3},{5,4},{6,5},{7,6},{9,8},{10,9},{11,10},{12... | collective-permute-start | bytes 11528 | tf_op jit(solution)/shard_map/ppermute | solution.py:25
  384.4 382.6 %all-reduce.7.cloned.1.call-start = ((), (), s32[]{:S(2)}) async-start(), calls=%async_computation | async-start | bytes 884736 | tf_op jit(solution)/shard_map/psum | solution.py:116
  397.4 121.0 %collective-permute-start.24 = (bf16[48,2,256]{0,1,2:T(2,128)(2,1)S(1)}, bf16[48,2,256]{0,1,2:T(2,128)(2,1)S(1)}, u32[]{:S(2)}, u32[]{:S(2)}) collective-permute-start(bf16[48,2,256]{0,1,2:T(2,128)(2,1)S(1)} %get-tuple-element.124), channel_id=1, source_target_pairs={{0,8},{8,16},{16,24},{1,9},{9,17},{17,25},{2,10},{10,18},{18,26},{... | collective-permute-start | bytes 147464 | tf_op jit(solution)/shard_map/ppermute | solution.py:22
  400.2 118.3 %collective-permute-start.25 = (bf16[48,2,256]{0,1,2:T(2,128)(2,1)S(1)}, bf16[48,2,256]{0,1,2:T(2,128)(2,1)S(1)}, u32[]{:S(2)}, u32[]{:S(2)}) collective-permute-start(bf16[48,2,256]{0,1,2:T(2,128)(2,1)S(1)} %get-tuple-element.125), channel_id=1, source_target_pairs={{8,0},{16,8},{24,16},{9,1},{17,9},{25,17},{10,2},{18,10},{26,18},{... | collective-permute-start | bytes 147464 | tf_op jit(solution)/shard_map/ppermute | solution.py:25
  518.9 14.3 %collective-permute-start.26 = (bf16[48,20,2]{2,0,1:T(8,128)(2,1)S(1)}, bf16[48,20,2]{2,0,1:T(8,128)(2,1)S(1)}, u32[]{:S(2)}, u32[]{:S(2)}) collective-permute-start(bf16[48,20,2]{2,0,1:T(8,128)(2,1)S(1)} %get-tuple-element.154), channel_id=1, source_target_pairs={{0,1},{1,2},{2,3},{3,4},{4,5},{5,6},{6,7},{8,9},{9,10},{10,11},{11... | collective-permute-start | bytes 11528 | tf_op jit(solution)/shard_map/ppermute | solution.py:22
  522.3 10.9 %collective-permute-start.27 = (bf16[48,20,2]{2,0,1:T(8,128)(2,1)S(1)}, bf16[48,20,2]{2,0,1:T(8,128)(2,1)S(1)}, u32[]{:S(2)}, u32[]{:S(2)}) collective-permute-start(bf16[48,20,2]{2,0,1:T(8,128)(2,1)S(1)} %get-tuple-element.155), channel_id=1, source_target_pairs={{1,0},{2,1},{3,2},{4,3},{5,4},{6,5},{7,6},{9,8},{10,9},{11,10},{12... | collective-permute-start | bytes 11528 | tf_op jit(solution)/shard_map/ppermute | solution.py:25
  572.5 14.4 %collective-permute-start.30 = (bf16[48,1,257]{0,1,2:T(2,128)(2,1)}, bf16[48,1,257]{0,1,2:T(2,128)(2,1)}, u32[]{:S(2)}, u32[]{:S(2)}) collective-permute-start(bf16[48,1,257]{0,1,2:T(2,128)(2,1)} %slice.527), channel_id=1, source_target_pairs={{8,0},{16,8},{24,16},{9,1},{17,9},{25,17},{10,2},{18,10},{26,18},{... | collective-permute-start | bytes 74024 | tf_op jit(solution)/shard_map/ppermute | solution.py:33
  594.0 8.5 %collective-permute-start.31 = (f32[48,16,1]{0,1,2:T(8,128)S(1)}, f32[48,16,1]{0,1,2:T(8,128)S(1)}, u32[]{:S(2)}, u32[]{:S(2)}) collective-permute-start(f32[48,16,1]{0,1,2:T(8,128)S(1)} %slice.419), channel_id=1, source_target_pairs={{1,0},{2,1},{3,2},{4,3},{5,4},{6,5},{7,6},{9,8},{10,9},{11,10},{12... | collective-permute-start | bytes 9224 | tf_op jit(solution)/shard_map/ppermute | solution.py:33
  613.1 21.7 %collective-permute-start.34 = (bf16[48,20,2]{2,0,1:T(8,128)(2,1)S(1)}, bf16[48,20,2]{2,0,1:T(8,128)(2,1)S(1)}, u32[]{:S(2)}, u32[]{:S(2)}) collective-permute-start(bf16[48,20,2]{2,0,1:T(8,128)(2,1)S(1)} %get-tuple-element.152), channel_id=1, source_target_pairs={{0,1},{1,2},{2,3},{3,4},{4,5},{5,6},{6,7},{8,9},{9,10},{10,11},{11... | collective-permute-start | bytes 11528 | tf_op jit(solution)/shard_map/ppermute | solution.py:22
  618.5 16.3 %collective-permute-start.35 = (bf16[48,20,2]{2,0,1:T(8,128)(2,1)S(1)}, bf16[48,20,2]{2,0,1:T(8,128)(2,1)S(1)}, u32[]{:S(2)}, u32[]{:S(2)}) collective-permute-start(bf16[48,20,2]{2,0,1:T(8,128)(2,1)S(1)} %get-tuple-element.153), channel_id=1, source_target_pairs={{1,0},{2,1},{3,2},{4,3},{5,4},{6,5},{7,6},{9,8},{10,9},{11,10},{12... | collective-permute-start | bytes 11528 | tf_op jit(solution)/shard_map/ppermute | solution.py:25
  (83 other events, 1546.8 us)
Sparse Core Ops, SparseCore 0:
  139.9 131.4 all-reduce.10
  384.5 130.5 all-reduce.8
  634.9 132.0 all-reduce.6
where the time goes:
time: 792 us; the launch traced here: 782 us
  waiting for transfers between devices  377 us (48%)
  local copies, waits for them, and re-layouts  163 us (21%)
  starting transfers between devices  96.1 us (12%)
  matrix products  89.8 us (11%)
  other arithmetic  35.4 us (4%)
  between operations  20.5 us (3%)
    psum x3, waiting for transfers between devices, body(): grad_one = lax.psum(grad_one, ('rows', 'cols'))  348 us
    transpose x6, matrix products, kernel_grad(): return jnp.transpose(summed, (1, 0, 2, 3))  62.4 us
    conv_general_dilated x33, local copies, waits for them, and re-layouts, plain_conv(): lax.conv_general_dilated(source[None], kernel, (stride, stride), 'VALID',...  54.5 us
    ppermute x12, starting transfers between devices, with_halo(): lax.ppermute(lax.slice_in_dim(block, block.shape[dim] - width, None, axis...  49.5 us
    broadcast_in_dim x15, local copies, waits for them, and re-layouts, plain_conv(): source[None]  32 us
    ppermute x12, starting transfers between devices, shifted(): return lax.ppermute(block, axis, route)  29.6 us
    unnamed x149, local copies, waits for them, and re-layouts  26.5 us
    conv_general_dilated x9, matrix products, plain_conv(): lax.conv_general_dilated(source[None], kernel, (stride, stride), 'VALID',...  23.4 us
  transfers between devices with their start and end apart: 39, of which 14 were waited for; matrix products, arithmetic and copies ran while one was open for 20% of the time, Pallas kernels for 0%

commit v1 on v0

v1 whole, which is shorter than its diff:
```python
import functools

import jax
import jax.numpy as jnp
import ml_dtypes
import numpy as np
from jax import lax
from jax.experimental import pallas as pl
from jax.experimental.pallas import tpu as pltpu
from jax.sharding import PartitionSpec as P

REPLAYS = 3

step_size = 0.5
clip_bound = 0.5
momentum_rate = 0.9
learn_rate = 0.005
mean_epsilon = 1e-06

MESH = pl.DeviceIdType.MESH
BF16 = jnp.bfloat16
F32 = jnp.float32
RIM = 3
LANES = 128
SECOND = 64
VMEM_LIMIT = 56 * 1024 * 1024
WHOLE = pl.BlockSpec(memory_space=pltpu.VMEM)


class Flat:
    def __init__(self, channels, rows, cols):
        self.channels, self.rows, self.cols = channels, rows, cols
        self.pitch = cols + 16
        self.total = -(-((rows + 2 * RIM) * self.pitch) // LANES) * LANES
        self.lift = rows * self.pitch
        self.edge = -(-(RIM * self.pitch) // LANES) * LANES
        first = RIM * self.pitch
        self.own_low = first // LANES * LANES
        self.own_high = -(-(first + self.lift) // LANES) * LANES
        self.down_from = self.own_low
        self.band = self.total - (self.down_from + self.lift)
        assert self.lift % LANES == 0 and self.edge <= self.band

    def at(self, row, col):
        return (row + RIM) * self.pitch + col + RIM

    def places(self):
        groups = []
        lane = 0
        for down, right in ((0, -1), (0, 1), (-1, -1), (-1, 1), (1, -1), (1, 1)):
            rows = {0: range(self.rows), -1: range(self.rows - RIM, self.rows), 1: range(RIM)}[down]
            cols = {-1: range(self.cols - RIM, self.cols), 1: range(RIM)}[right]
            pairs = [(r, c) for r in rows for c in cols]
            groups.append(((down, right), lane, pairs))
            lane += len(pairs)
        assert lane <= LANES
        return groups

    def tables(self):
        pack = np.zeros((self.total, LANES), ml_dtypes.bfloat16)
        unpack = np.zeros((LANES, self.total), ml_dtypes.bfloat16)
        for (down, right), lane, pairs in self.places():
            for k, (r, c) in enumerate(pairs):
                pack[self.at(r, c), lane + k] = 1
                unpack[lane + k, self.at(r + down * self.rows, c + right * self.cols)] = 1
        spots = np.arange(self.total)
        where = np.zeros((8, self.total), np.int32)
        where[0] = spots // self.pitch - RIM
        where[1] = spots % self.pitch - RIM
        return pack, unpack, where


def position(axis, distance):
    count = lax.axis_size(axis)
    return lax.rem(lax.axis_index(axis) + (distance + count), count)


def beside_of(down, right):
    return {"rows": position("rows", down), "cols": position("cols", right)}


STEPS = ((0, -1), (0, 1), (-1, -1), (-1, 1), (1, -1), (1, 1))


def exchange_kernel(flat, row_count, col_count, with_sum, with_rim, *refs):
    refs = list(refs)
    if with_rim:
        own, packed = refs.pop(0), refs.pop(0)
    if with_sum:
        grad = refs.pop(0)
    if with_rim:
        above, below, beside = refs.pop(0), refs.pop(0), refs.pop(0)
    if with_sum:
        summed, part_rows, part_cols, half = refs[:4]
        refs = refs[4:]
    sends, recvs = refs

    me_row, me_col = lax.axis_index("rows"), lax.axis_index("cols")
    barrier = pltpu.get_barrier_semaphore()
    greeted = 0
    if with_sum:
        for d in range(1, row_count):
            pl.semaphore_signal(barrier, inc=1, device_id=beside_of(d, 0), device_id_type=MESH)
            greeted += 1
        for d in range(1, col_count):
            pl.semaphore_signal(barrier, inc=1, device_id=beside_of(0, d), device_id_type=MESH)
            greeted += 1
    if with_rim:
        also = [s for s in STEPS if not with_sum or 0 not in s]
        if not with_sum:
            also += [(-1, 0), (1, 0)]
        for down, right in also:
            pl.semaphore_signal(barrier, inc=1, device_id=beside_of(down, right), device_id_type=MESH)
            greeted += 1
    pl.semaphore_wait(barrier, greeted)

    used = [0]

    def send(source, target, device):
        k = used[0]
        used[0] += 1
        copy = pltpu.make_async_remote_copy(
            src_ref=source,
            dst_ref=target,
            send_sem=sends.at[k],
            recv_sem=recvs.at[k],
            device_id=device,
            device_id_type=MESH,
        )
        copy.start()
        return copy

    rim_copies = []
    first_copies = []
    if with_sum:
        tall = grad.shape[0] // row_count
        short = tall // col_count
        for d in range(1, row_count):
            there = position("rows", d)
            first_copies.append(
                send(grad.at[pl.ds(there * tall, tall)], part_rows.at[d - 1], beside_of(d, 0))
            )
    if with_rim:
        low, high = flat.lift, flat.lift + flat.edge
        rim_copies.append(send(own.at[:, :, low:high], above, beside_of(1, 0)))
        low, high = flat.down_from, flat.down_from + flat.band
        rim_copies.append(send(own.at[:, :, low:high], below, beside_of(-1, 0)))
        for k, (down, right) in enumerate(STEPS):
            rim_copies.append(send(packed, beside.at[k], beside_of(-down, -right)))
    if with_sum:
        for copy in first_copies:
            copy.wait()
        total = grad[pl.ds(me_row * tall, tall)]
        for d in range(1, row_count):
            total = total + part_rows[d - 1]
        half[...] = total
        second_copies = []
        for d in range(1, col_count):
            there = position("cols", d)
            second_copies.append(
                send(half.at[pl.ds(there * short, short)], part_cols.at[d - 1], beside_of(0, d))
            )
        for copy in second_copies:
            copy.wait()
        total = half[pl.ds(me_col * short, short)]
        for d in range(1, col_count):
            total = total + part_cols[d - 1]
        mine = pl.ds(me_row * tall + me_col * short, short)
        summed[mine] = total
        third_copies = []
        for d in range(1, col_count):
            third_copies.append(send(summed.at[mine], summed.at[mine], beside_of(0, d)))
        for copy in third_copies:
            copy.wait()
        band = pl.ds(me_row * tall, tall)
        last_copies = []
        for d in range(1, row_count):
            last_copies.append(send(summed.at[band], summed.at[band], beside_of(d, 0)))
        for copy in last_copies:
            copy.wait()
    for copy in rim_copies:
        copy.wait()


def exchange(flat, call_id, own=None, packed=None, grad=None):
    row_count, col_count = lax.axis_size("rows"), lax.axis_size("cols")
    operands, shapes, scratch = [], [], []
    count = 0
    if own is not None:
        operands += [own, packed]
        planes = own.shape[0]
        shapes += [
            jax.ShapeDtypeStruct((planes, flat.channels, flat.edge), BF16),
            jax.ShapeDtypeStruct((planes, flat.channels, flat.band), BF16),
            jax.ShapeDtypeStruct((len(STEPS),) + packed.shape, BF16),
        ]
        count += 8
    if grad is not None:
        operands.append(grad)
        shapes.append(jax.ShapeDtypeStruct(grad.shape, F32))
        tall = grad.shape[0] // row_count
        short = tall // col_count
        scratch += [
            pltpu.VMEM((row_count - 1, tall, LANES), F32),
            pltpu.VMEM((col_count - 1, short, LANES), F32),
            pltpu.VMEM((tall, LANES), F32),
        ]
        count += 2 * (row_count - 1) + 2 * (col_count - 1)
    return pl.pallas_call(
        functools.partial(
            exchange_kernel, flat, row_count, col_count, grad is not None, own is not None
        ),
        out_shape=shapes,
        in_specs=[WHOLE] * len(operands),
        out_specs=[WHOLE] * len(shapes),
        scratch_shapes=scratch + [pltpu.SemaphoreType.DMA((count,)), pltpu.SemaphoreType.DMA((count,))],
        compiler_params=pltpu.CompilerParams(
            collective_id=call_id, has_side_effects=True, vmem_limit_bytes=VMEM_LIMIT
        ),
    )(*operands)


def dot(a, b):
    return jnp.dot(a, b, preferred_element_type=F32)


def dot_nt(a, b):
    return lax.dot_general(a, b, (((1,), (1,)), ((), ())), preferred_element_type=F32)


def updated(state, moment, grad, entries):
    lane = lax.broadcasted_iota(jnp.int32, (1, LANES), 1)
    squared = jnp.sum(grad * grad, axis=0, keepdims=True)
    one = jnp.sum(jnp.where(lane < SECOND, squared, 0.0), axis=1, keepdims=True) / entries
    two = jnp.sum(jnp.where(lane >= SECOND, squared, 0.0), axis=1, keepdims=True) / entries
    scale = jnp.sqrt(jnp.where(lane < SECOND, one, two) + mean_epsilon)
    moment = momentum_rate * moment + grad / scale
    return state - learn_rate * moment, moment


def rolled(values, shift):
    if shift == 0:
        return values
    return pltpu.roll(values, (-shift) % values.shape[1], axis=1)


def merged_rim(flat, own, above, below, beside, unpack, index):
    return own


def step_kernel(flat, row_count, col_count, first, *refs):
    refs = list(refs)
    own, above, below, beside, image, perturb, state, moment = refs[:8]
    refs = refs[8:]
    if first:
        pack, unpack, where = refs[:3]
        refs = refs[3:]
        new_perturb, new_own, new_packed, new_grad, predict_out, target_out = refs[:6]
        refs = refs[6:]
    else:
        grad, target_in, pack, unpack, where = refs[:5]
        refs = refs[5:]
        new_perturb, new_own, new_packed, new_grad, predict_out, new_state, new_moment = refs[:7]
        refs = refs[7:]
    ext, attacked_cols, slope, hidden, hidden_cols, rest_cols, pre_cols, pre, wide, back, spread_weight = refs
    C, N, T = flat.channels, flat.total, flat.pitch
    taps = [(a, b) for a in range(3) for b in range(3)]
    K = 9 * C
    low, high = flat.own_low, flat.own_high

    me_row, me_col = lax.axis_index("rows"), lax.axis_index("cols")
    row, col = where[0:1, :], where[1:2, :]
    owned = ((row >= 0) & (row < flat.rows) & (col >= 0) & (col < flat.cols)).astype(F32)
    far_row, far_col = row + me_row * flat.rows, col + me_col * flat.cols
    inside = (
        (far_row >= 0)
        & (far_row < flat.rows * row_count)
        & (far_col >= 0)
        & (far_col < flat.cols * col_count)
    ).astype(F32)

    if first:
        now = state[...]
    else:
        now, later = updated(state[...], moment[...], grad[0:K, :], K * C)
        new_state[...] = now
        new_moment[...] = later
    fast = now.astype(BF16)
    eye = (
        lax.broadcasted_iota(jnp.int32, (LANES, LANES), 0)
        == lax.broadcasted_iota(jnp.int32, (LANES, LANES), 1)
    ).astype(F32).astype(BF16)
    ahead = dot_nt(eye, fast).astype(BF16)
    ahead_one, ahead_two = ahead[0:C, :], ahead[SECOND : SECOND + C, :]
    from_lane = lax.broadcasted_iota(jnp.int32, (LANES, K), 0)
    to_lane = lax.broadcasted_iota(jnp.int32, (LANES, K), 1)
    back_one = jnp.zeros((C, K), F32)
    for k in range(9):
        put = ((to_lane == from_lane + k * C) & (from_lane < C)).astype(F32).astype(BF16)
        back_one = back_one + dot(fast[k * C : (k + 1) * C, :], put)
    back_one = back_one.astype(BF16)
    four = 4 * C
    from_lane = lax.broadcasted_iota(jnp.int32, (LANES, four), 0)
    to_lane = lax.broadcasted_iota(jnp.int32, (LANES, four), 1)
    for py in range(2):
        for px in range(2):
            block = jnp.zeros((C, four), F32)
            for a, dy in ([(1, 0)] if py == 0 else [(0, 1), (2, 0)]):
                for b, dx in ([(1, 0)] if px == 0 else [(0, 1), (2, 0)]):
                    k = 3 * a + b
                    slot = 2 * dy + dx
                    put = (
                        (to_lane == from_lane - SECOND + slot * C)
                        & (from_lane >= SECOND)
                        & (from_lane < SECOND + C)
                    ).astype(F32).astype(BF16)
                    block = block + dot(fast[k * C : (k + 1) * C, :], put)
            spread_weight[(2 * py + px) * C : (2 * py + px + 1) * C, :] = block.astype(BF16)

    planes = own.shape[0]
    lane = lax.broadcasted_iota(jnp.int32, (1, LANES), 1)
    gathered = jnp.zeros((planes * C, LANES), F32)
    for k, ((down, right), start, pairs) in enumerate(flat.places()):
        there_row, there_col = me_row + down, me_col + right
        exists = (
            (there_row >= 0) & (there_row < row_count) & (there_col >= 0) & (there_col < col_count)
        )
        keep = (lane >= start) & (lane < start + len(pairs)) & exists
        gathered = gathered + jnp.where(keep, beside[k].astype(F32), 0.0)
    gathered = gathered.astype(BF16)
    has_above = jnp.where(me_row > 0, 1.0, 0.0).astype(F32)
    has_below = jnp.where(me_row < row_count - 1, 1.0, 0.0).astype(F32)
    end = flat.down_from + flat.lift
    for p in range(planes):
        ext[...] = own[p].astype(F32) + dot(gathered[p * C : (p + 1) * C, :], unpack[...])
        ext[:, 0 : flat.edge] += above[p].astype(F32) * has_above
        ext[:, end:N] += below[p].astype(F32) * has_below
        if p == 4:
            target_out[...] = ext[...].astype(BF16)
            continue
        full = ext[...]
        for k, (a, b) in enumerate(taps):
            moved = rolled(full, (a - 1) * T + (b - 1))
            attacked_cols[p, k * C : (k + 1) * C, :] = moved.astype(BF16)
        pre_value = dot(ahead_one, attacked_cols[p])
        sigmoid_value = jax.nn.sigmoid(pre_value)
        hidden[p] = pre_value * sigmoid_value * inside
        slope[p] = sigmoid_value * (1.0 + pre_value * (1.0 - sigmoid_value)) * inside
    target = (target_out if first else target_in)[...].astype(F32)

    for k, (a, b) in enumerate(taps):
        py, dy = [(1, -1), (0, 0), (1, 0)][a]
        px, dx = [(1, -1), (0, 0), (1, 0)][b]
        hidden_cols[k * C : (k + 1) * C, :] = rolled(hidden[2 * py + px], dy * T + dx).astype(BF16)
    predict = dot(ahead_two, hidden_cols[...])
    predict_out[...] = predict.astype(BF16)
    residual = (predict - target) * inside
    wide[...] = jnp.zeros(wide.shape, BF16)
    wide[SECOND : SECOND + C, :] = (residual * owned)[:, low:high].astype(BF16)
    total = dot_nt(hidden_cols[:, low:high], wide[...])
    wide[...] = jnp.zeros(wide.shape, BF16)
    for k, shift in enumerate((0, 1, T, T + 1)):
        rest_cols[k * C : (k + 1) * C, :] = rolled(residual, shift).astype(BF16)
    hidden_grad = dot(spread_weight[...], rest_cols[...])
    new_own[...] = jnp.zeros(new_own.shape, BF16)
    new_perturb[...] = jnp.zeros(new_perturb.shape, F32)
    for p in range(4):
        pre_grad = hidden_grad[p * C : (p + 1) * C, :] * slope[p]
        wide[0:C, :] = (pre_grad * owned)[:, low:high].astype(BF16)
        total = total + dot_nt(attacked_cols[p, :, low:high], wide[...])
        for k, (a, b) in enumerate(taps):
            moved = rolled(pre_grad, -((a - 1) * T + (b - 1)))
            pre_cols[k * C : (k + 1) * C, :] = moved[:, low:high].astype(BF16)
        input_grad = dot(back_one, pre_cols[...])
        moved = jnp.clip(
            perturb[p, :, low:high] + step_size * jnp.tanh(input_grad), -clip_bound, clip_bound
        )
        moved = moved * owned[:, low:high]
        new_perturb[p, :, low:high] = moved
        attacked = (image[p, :, low:high].astype(F32) + moved).astype(BF16)
        new_own[p, :, low:high] = attacked
        new_packed[p * C : (p + 1) * C, :] = dot(attacked, pack[low:high, :]).astype(BF16)
    new_grad[...] = jnp.zeros(new_grad.shape, F32)
    new_grad[0:K, :] = total


def step(flat, tables, own, rim, image, perturb, state, moment, grad, target, tall):
    first = grad is None
    C, N = flat.channels, flat.total
    K = 9 * C
    operands = [own, *rim, image, perturb, state, moment]
    if not first:
        operands += [grad, target]
    operands += list(tables)
    shapes = [
        jax.ShapeDtypeStruct((4, C, N), F32),
        jax.ShapeDtypeStruct((4, C, N), BF16),
        jax.ShapeDtypeStruct((4 * C, LANES), BF16),
        jax.ShapeDtypeStruct((tall, LANES), F32),
        jax.ShapeDtypeStruct((C, N), BF16),
    ]
    if first:
        shapes.append(jax.ShapeDtypeStruct((C, N), BF16))
    else:
        shapes += [jax.ShapeDtypeStruct((K, LANES), F32)] * 2
    width = flat.own_high - flat.own_low
    scratch = [
        pltpu.VMEM((C, N), F32),
        pltpu.VMEM((4, K, N), BF16),
        pltpu.VMEM((4, C, N), F32),
        pltpu.VMEM((4, C, N), F32),
        pltpu.VMEM((K, N), BF16),
        pltpu.VMEM((4 * C, N), BF16),
        pltpu.VMEM((K, width), BF16),
        pltpu.VMEM((C, N), F32),
        pltpu.VMEM((LANES, width), BF16),
        pltpu.VMEM((C, K), BF16),
        pltpu.VMEM((4 * C, 4 * C), BF16),
    ]
    return pl.pallas_call(
        functools.partial(step_kernel, flat, lax.axis_size("rows"), lax.axis_size("cols"), first),
        out_shape=shapes,
        in_specs=[WHOLE] * len(operands),
        out_specs=[WHOLE] * len(shapes),
        scratch_shapes=scratch,
        compiler_params=pltpu.CompilerParams(vmem_limit_bytes=VMEM_LIMIT),
    )(*operands)


def last_kernel(entries, state, moment, grad, new_state, new_moment):
    now, later = updated(state[...], moment[...], grad[0 : state.shape[0], :], entries)
    new_state[...] = now
    new_moment[...] = later


def parted(flat, block):
    C, h, w = flat.channels, flat.rows, flat.cols
    order = np.zeros((2 * w, 2 * w), np.float32)
    for c in range(w):
        order[2 * c, c] = 1
        order[2 * c + 1, w + c] = 1
    order = jnp.asarray(order, block.dtype)
    sorted_cols = jnp.dot(
        block.reshape(C * 2 * h, 2 * w),
        order,
        precision=lax.Precision.HIGHEST if block.dtype == F32 else None,
        preferred_element_type=block.dtype,
    )
    planes = sorted_cols.reshape(C, h, 2, 2, w).transpose(2, 3, 0, 1, 4).reshape(4, C, h, w)
    return laid(flat, planes)


def laid(flat, planes):
    count = planes.shape[0]
    right = flat.pitch - flat.cols - RIM
    planes = jnp.pad(planes, ((0, 0), (0, 0), (RIM, RIM), (RIM, right)))
    planes = planes.reshape(count, flat.channels, -1)
    return jnp.pad(planes, ((0, 0), (0, 0), (0, flat.total - planes.shape[2])))


def unlaid(flat, planes):
    count = planes.shape[0]
    planes = planes[:, :, : (flat.rows + 2 * RIM) * flat.pitch]
    planes = planes.reshape(count, flat.channels, flat.rows + 2 * RIM, flat.pitch)
    return planes[:, :, RIM : RIM + flat.rows, RIM : RIM + flat.cols]


def joined(flat, planes):
    C, h, w = flat.channels, flat.rows, flat.cols
    order = np.zeros((2 * w, 2 * w), np.float32)
    for c in range(w):
        order[c, 2 * c] = 1
        order[w + c, 2 * c + 1] = 1
    blocks = unlaid(flat, planes).reshape(2, 2, C, h, w).transpose(2, 3, 0, 1, 4)
    blocks = jnp.dot(
        blocks.reshape(C * 2 * h, 2 * w), jnp.asarray(order), precision=lax.Precision.HIGHEST
    )
    return blocks.reshape(C, 2 * h, 2 * w)


def stacked(one, two):
    C = one.shape[0]
    one, two = (k.transpose(2, 3, 1, 0).reshape(9 * C, C) for k in (one, two))
    one = jnp.pad(one, ((0, 0), (0, SECOND - C)))
    two = jnp.pad(two, ((0, 0), (0, SECOND - C)))
    return jnp.concatenate([one, two], axis=1)


def unstacked(both, C):
    return tuple(
        both[:, low : low + C].reshape(3, 3, C, C).transpose(3, 2, 0, 1) for low in (0, SECOND)
    )


def body(image, perturb, target, kernel_one, kernel_two, moment_one, moment_two):
    C = image.shape[0]
    flat = Flat(C, target.shape[1], target.shape[2])
    tables = tuple(jnp.asarray(t) for t in flat.tables())
    devices = lax.axis_size("rows") * lax.axis_size("cols")
    tall = -(-9 * C // (8 * devices)) * 8 * devices
    image = parted(flat, image)
    perturb = parted(flat, perturb)
    state = stacked(kernel_one, kernel_two)
    moment = stacked(moment_one, moment_two)
    own = (image.astype(F32) + perturb).astype(BF16)
    own = jnp.concatenate([own, laid(flat, target[None])], axis=0)
    packed = jnp.dot(
        own.reshape(5 * C, flat.total), tables[0], preferred_element_type=F32
    ).astype(BF16)
    rim = exchange(flat, 0, own, packed)
    grad = None
    held_target = None
    for replay in range(REPLAYS):
        results = step(
            flat, tables, own, rim, image, perturb, state, moment, grad, held_target, tall
        )
        perturb, own, packed, grad, predict = results[:5]
        if replay == 0:
            held_target = results[5]
        else:
            state, moment = results[5:]
        if replay < REPLAYS - 1:
            *rim, grad = exchange(flat, 1, own, packed, grad)
        else:
            (grad,) = exchange(flat, 2, grad=grad)
    state, moment = pl.pallas_call(
        functools.partial(last_kernel, 9 * C * C),
        out_shape=[jax.ShapeDtypeStruct(state.shape, F32)] * 2,
        in_specs=[WHOLE] * 3,
        out_specs=[WHOLE] * 2,
    )(state, moment, grad)
    new_one, new_two = unstacked(state, C)
    new_moment_one, new_moment_two = unstacked(moment, C)
    prediction = unlaid(flat, predict[None])[0]
    return (joined(flat, perturb), prediction, new_one, new_two, new_moment_one, new_moment_two)


def solution(mesh):
    in_specs = (
        P(None, "rows", "cols"),
        P(None, "rows", "cols"),
        P(None, "rows", "cols"),
        P(),
        P(),
        P(),
        P(),
    )
    out_specs = (P(None, "rows", "cols"), P(None, "rows", "cols"), P(), P(), P(), P())
    return jax.shard_map(body, mesh=mesh, in_specs=in_specs, out_specs=out_specs, check_vma=False)
```

time: 792 us -> 160 us (0.20); the launches traced: 782 us -> 159 us
  waiting for transfers between devices: 377 us -> 0 us
  local copies, waits for them, and re-layouts: 163 us -> 29.6 us
  Pallas kernels: 0 us -> 121 us
  starting transfers between devices: 96.1 us -> 0 us
  matrix products: 89.8 us -> 3.82 us
  other arithmetic: 35.4 us -> 4.09 us
  between operations: 20.5 us -> 0.89 us
    psum x3 -> x0, waiting for transfers between devices: 348 us -> none  [body(): grad_one = lax.psum(grad_one, ('rows', 'cols'))]
    pallas_call x0 -> x8, Pallas kernels: none -> 121 us  [the longest x4 84.4 us: exchange(): pl.pallas_call(functools.partial(exchange_kernel, flat, row_count, col_co...]
    ppermute x36 -> x0, starting transfers between devices: 95.4 us -> none  [the longest x12 49.5 us: with_halo(): lax.ppermute(lax.slice_in_dim(block, block.shape[dim] - width, None, axis...]
    transpose x6 -> x0, matrix products: 62.4 us -> none  [kernel_grad(): return jnp.transpose(summed, (1, 0, 2, 3))]
    conv_general_dilated x42 -> x0, local copies, waits for them, and re-layouts: 57.2 us -> none  [the longest x33 54.5 us: plain_conv(): lax.conv_general_dilated(source[None], kernel, (stride, stride), 'VALID',...]
    broadcast_in_dim x18 -> x0, local copies, waits for them, and re-layouts: 32.2 us -> none  [the longest x15 32 us: plain_conv(): source[None]]
    ppermute x36 -> x0, waiting for transfers between devices: 29 us -> none  [the longest x12 18.7 us: with_halo(): lax.ppermute(lax.slice_in_dim(block, block.shape[dim] - width, None, axis...]
    conv_general_dilated x12 -> x0, matrix products: 27.4 us -> none  [the longest x9 23.4 us: plain_conv(): lax.conv_general_dilated(source[None], kernel, (stride, stride), 'VALID',...]
  transfers between devices with their start and end apart: 39 -> 0, of which waited for: 14 -> 0; matrix products, arithmetic and copies ran while one was open for 20% -> 0% of each run, Pallas kernels for 0% -> 0%
where the time goes in v1:
time: 160 us; the launch traced here: 159 us
  Pallas kernels  121 us (76%)
  local copies, waits for them, and re-layouts  29.6 us (18%)
  other arithmetic  4.09 us (3%)
  matrix products  3.82 us (2%)
    pallas_call x4, Pallas kernels, exchange(): pl.pallas_call(functools.partial(exchange_kernel, flat, row_count, col_co...  84.4 us
    pallas_call x3, Pallas kernels, step(): pl.pallas_call(functools.partial(step_kernel, flat, lax.axis_size('rows')...  34.3 us
    reshape x3, local copies, waits for them, and re-layouts, laid(): planes = planes.reshape(count, flat.channels, -1)  5.67 us
    reshape x2, local copies, waits for them, and re-layouts, unlaid(): planes.reshape(count, flat.channels, flat.rows + 2 * RIM, flat.pitch)  4.82 us
    transpose x4, local copies, waits for them, and re-layouts, stacked(): one, two = (k.transpose(2, 3, 1, 0).reshape(9 * C, C) for k in (one, two))  4.32 us
    reshape x4, local copies, waits for them, and re-layouts, unstacked(): both[:, low:low + C].reshape(3, 3, C, C).transpose(3, 2, 0, 1)  3.52 us

profile of v1, /device:TPU:0, one launch (start us, length us, event | category | flops | bytes accessed | tf_op | source)
XLA Modules:
  0.0 159.2 jit_solution(13937697742786700609)
XLA Ops:
  0.6 1.1 copy.34
  1.8 1.1 copy.35
  2.8 1.1 copy.36
  3.9 1.1 copy.37
  5.0 0.9 select_maximum_fusion
  8.8 1.3 copy.33
  11.0 2.3 %reshape.78 = bf16[4,48,2016]{2,1,0:T(8,128)(2,1)S(1)} reshape(bf16[4,48,14,144]{3,2,1,0:T(8,128)(2,1)S(1)} %pad.37) | data formatting | bytes 1548288 | tf_op jit(solution)/shard_map/reshape | solution.py:457
  16.5 2.9 %reshape.80 = f32[4,48,2016]{2,1,0:T(8,128)} reshape(f32[4,48,14,144]{3,2,1,0:T(8,128)S(1)} %pad.39) | data formatting | bytes 3096576 | tf_op jit(solution)/shard_map/reshape | solution.py:457
  19.4 3.1 %fusion.2 = (f32[4,48,2048]{2,1,0:T(8,128)}, bf16[4,48,2048]{2,1,0:T(8,128)(2,1)S(1)}) fusion(f32[4,48,2016]{2,1,0:T(8,128)} %reshape.80, bf16[4,48,2016]{2,1,0:T(8,128)(2,1)} %copy-done.2), kind=kLoop, calls=%fused_computation.13 | loop fusion | flops 1179648 | bytes 4681728 | tf_op jit(solution)/shard_map/jit(_pad)/pad | solution.py:458
  22.6 1.1 copy-done.1
  23.7 1.0 convolution_convert_fusion.refs_1_
  24.7 17.3 %shard_map.172 = (bf16[5,48,512]{2,1,0:T(8,128)(2,1)}, bf16[5,48,512]{2,1,0:T(8,128)(2,1)}, bf16[6,240,128]{2,1,0:T(8,128)(2,1)}) custom-call(bf16[5,48,2048]{2,1,0:T(8,128)(2,1)} %copy-done, bf16[240,128]{1,0:T(8,128)(2,1)} %convolution_convert_fusion.refs_1_), custom_call_target="tpu_custom_call" | custom-call | tf_op jit(solution)/shard_map/pallas_call | solution.py:209
  41.9 11.3 %shard_map.173 = (f32[4,48,2048]{2,1,0:T(8,128)}, bf16[4,48,2048]{2,1,0:T(8,128)(2,1)}, bf16[192,128]{1,0:T(8,128)(2,1)}, f32[512,128]{1,0:T(8,128)}, bf16[48,20...) custom-call(bf16[5,48,2048]{2,1,0:T(8,128)(2,1)} %copy-done, bf16[5,48,512]{2,1,0:T(8,128)(2,1)} %get-tuple-element.35.refs_1_, ...), custom_call_target="tpu_custom_call" | custom-call | tf_op jit(solution)/shard_map/pallas_call | solution.py:420
  53.3 23.2 %shard_map.174 = (bf16[4,48,512]{2,1,0:T(8,128)(2,1)}, bf16[4,48,512]{2,1,0:T(8,128)(2,1)}, bf16[6,192,128]{2,1,0:T(8,128)(2,1)}, f32[512,128]{1,0:T(8,128)}) custom-call(bf16[4,48,2048]{2,1,0:T(8,128)(2,1)} %get-tuple-element.38.refs_0_, bf16[192,128]{1,0:T(8,128)(2,1)} %get-tuple-element.39.refs_1_, f32[512,128]{1,0:T(8,128)} %get-tuple-element.40.refs_2_), custom_call_target="tpu_custom_call" | custom-call | tf_op jit(solution)/shard_map/pallas_call | solution.py:209
  76.5 11.6 %shard_map.175 = (f32[4,48,2048]{2,1,0:T(8,128)}, bf16[4,48,2048]{2,1,0:T(8,128)(2,1)}, bf16[192,128]{1,0:T(8,128)(2,1)}, f32[512,128]{1,0:T(8,128)}, bf16[48,20...) custom-call(bf16[4,48,2048]{2,1,0:T(8,128)(2,1)} %get-tuple-element.38.refs_0_, ...), custom_call_target="tpu_custom_call" | custom-call | tf_op jit(solution)/shard_map/pallas_call | solution.py:420
  88.1 23.3 %shard_map.176 = (bf16[4,48,512]{2,1,0:T(8,128)(2,1)}, bf16[4,48,512]{2,1,0:T(8,128)(2,1)}, bf16[6,192,128]{2,1,0:T(8,128)(2,1)}, f32[512,128]{1,0:T(8,128)}) custom-call(bf16[4,48,2048]{2,1,0:T(8,128)(2,1)} %get-tuple-element.47.refs_0_, bf16[192,128]{1,0:T(8,128)(2,1)} %get-tuple-element.48.refs_1_, f32[512,128]{1,0:T(8,128)} %get-tuple-element.49.refs_2_), custom_call_target="tpu_custom_call" | custom-call | tf_op jit(solution)/shard_map/pallas_call | solution.py:209
  111.4 11.4 %shard_map.177 = (f32[4,48,2048]{2,1,0:T(8,128)}, bf16[4,48,2048]{2,1,0:T(8,128)(2,1)}, bf16[192,128]{1,0:T(8,128)(2,1)}, f32[512,128]{1,0:T(8,128)}, bf16[48,20...) custom-call(bf16[4,48,2048]{2,1,0:T(8,128)(2,1)} %get-tuple-element.47.refs_0_, ...), custom_call_target="tpu_custom_call" | custom-call | tf_op jit(solution)/shard_map/pallas_call | solution.py:420
  122.8 1.5 reshape.89
  125.1 20.6 %shard_map.178.grad = f32[512,128]{1,0:T(8,128)} custom-call(f32[512,128]{1,0:T(8,128)} %get-tuple-element.61.refs_0_), custom_call_target="tpu_custom_call" | custom-call | tf_op jit(solution)/shard_map/pallas_call | solution.py:209
  145.7 2.1 %shard_map.179 = (f32[432,128]{1,0:T(8,128)}, f32[432,128]{1,0:T(8,128)}) custom-call(f32[432,128]{1,0:T(8,128)} %get-tuple-element.59.state, f32[432,128]{1,0:T(8,128)} %get-tuple-element.60.moment, f32[512,128]{1,0:T(8,128)} %shard_map.178.grad), custom_call_target="tpu_custom_call" | custom-call | tf_op jit(solution)/shard_map/pallas_call | solution.py:526
  147.8 1.2 fusion.4
  151.6 1.1 copy.41
  152.7 3.3 %reshape.87 = f32[4,48,14,144]{3,2,1,0:T(8,128)S(1)} reshape(f32[4,48,2016]{2,1,0:T(8,128)} %bitcast.61) | data formatting | bytes 3096576 | tf_op jit(solution)/shard_map/reshape | solution.py:464
  157.6 1.7 %fusion.5 = f32[48,16,256]{2,1,0:T(8,128)} fusion(f32[48,16,256]{2,1,0:T(8,128)S(1)} %dot_general.35, f32[256,256,1]{1,0,2:T(8,128)S(1)} %copy-done.7), kind=kOutput, calls=%fused_computation.16 | convolution fusion | flops 603979776 | bytes 1835008 | tf_op jit(solution)/shard_map/dot_general | solution.py:475
  (40 shorter events, 11.8 us)
Async XLA Ops:
  0.6 5.3 %copy-start.6 = (bf16[48,16,256]{2,1,0:T(8,128)(2,1)S(1)}, bf16[48,16,256]{2,1,0:T(8,128)(2,1)}, u32[]{:S(2)}) copy-start(bf16[48,16,256]{2,1,0:T(8,128)(2,1)} %param.13) | copy-start | bytes 1179652
  2.8 3.3 %copy-start.9 = (bf16[2,128,256,1,1]{2,1,4,3,0:T(8,128)(2,1)S(1)}, bf16[2,128,256,1,1]{2,1,4,3,0:T(8,128)(2,1)}, u32[]{:S(2)}) copy-start(bf16[2,128,256,1,1]{2,1,4,3,0:T(8,128)(2,1)} %constant.47) | copy-start | bytes 393220
  5.9 0.9 copy-start.10
  6.1 1.5 copy-start.5
  6.4 1.6 %copy-start.8 = (f32[2,128,256,1,1]{2,1,4,3,0:T(8,128)S(1)}, f32[2,128,256,1,1]{2,1,4,3,0:T(8,128)}, u32[]{:S(2)}) copy-start(f32[2,128,256,1,1]{2,1,4,3,0:T(8,128)} %constant.48) | copy-start | bytes 786436
  13.3 0.9 copy-start.2
  14.2 1.4 copy-start.3
  22.5 1.2 copy-start.1
  22.6 2.1 %copy-start = (bf16[5,48,2048]{2,1,0:T(8,128)(2,1)}, bf16[5,48,2048]{2,1,0:T(8,128)(2,1)S(1)}, u32[]{:S(2)}) copy-start(bf16[5,48,2048]{2,1,0:T(8,128)(2,1)S(1)} %fusion.1.refs_0_) | copy-start | bytes 2949124
  147.8 2.8 %copy-start.4 = (f32[432,128]{1,0:T(8,128)S(1)}, f32[432,128]{1,0:T(8,128)}, u32[]{:S(2)}) copy-start(f32[432,128]{1,0:T(8,128)} %get-tuple-element.63) | copy-start | bytes 663556
  156.3 1.3 copy-start.7

commit v2 on v0

v2 whole, which is shorter than its diff:
```python
import functools

import jax
import jax.numpy as jnp
import ml_dtypes
import numpy as np
from jax import lax
from jax.experimental import pallas as pl
from jax.experimental.pallas import tpu as pltpu
from jax.sharding import PartitionSpec as P

REPLAYS = 3

step_size = 0.5
clip_bound = 0.5
momentum_rate = 0.9
learn_rate = 0.005
mean_epsilon = 1e-06

MESH = pl.DeviceIdType.MESH
BF16 = jnp.bfloat16
F32 = jnp.float32
RIM = 3
LANES = 128
SECOND = 64
VMEM_LIMIT = 56 * 1024 * 1024
WHOLE = pl.BlockSpec(memory_space=pltpu.VMEM)


class Flat:
    def __init__(self, channels, rows, cols):
        self.channels, self.rows, self.cols = channels, rows, cols
        self.pitch = cols + 16
        self.total = -(-((rows + 2 * RIM) * self.pitch) // LANES) * LANES
        self.lift = rows * self.pitch
        self.edge = -(-(RIM * self.pitch) // LANES) * LANES
        first = RIM * self.pitch
        self.own_low = first // LANES * LANES
        self.own_high = -(-(first + self.lift) // LANES) * LANES
        self.down_from = self.own_low
        self.band = self.total - (self.down_from + self.lift)
        assert self.lift % LANES == 0 and self.edge <= self.band

    def at(self, row, col):
        return (row + RIM) * self.pitch + col + RIM

    def places(self):
        groups = []
        lane = 0
        for down, right in ((0, -1), (0, 1), (-1, -1), (-1, 1), (1, -1), (1, 1)):
            rows = {0: range(self.rows), -1: range(self.rows - RIM, self.rows), 1: range(RIM)}[down]
            cols = {-1: range(self.cols - RIM, self.cols), 1: range(RIM)}[right]
            pairs = [(r, c) for r in rows for c in cols]
            groups.append(((down, right), lane, pairs))
            lane += len(pairs)
        assert lane <= LANES
        return groups

    def tables(self):
        pack = np.zeros((self.total, LANES), ml_dtypes.bfloat16)
        unpack = np.zeros((LANES, self.total), ml_dtypes.bfloat16)
        for (down, right), lane, pairs in self.places():
            for k, (r, c) in enumerate(pairs):
                pack[self.at(r, c), lane + k] = 1
                unpack[lane + k, self.at(r + down * self.rows, c + right * self.cols)] = 1
        spots = np.arange(self.total)
        where = np.zeros((8, self.total), np.int32)
        where[0] = spots // self.pitch - RIM
        where[1] = spots % self.pitch - RIM
        return pack, unpack, where


def position(axis, distance):
    count = lax.axis_size(axis)
    return lax.rem(lax.axis_index(axis) + (distance + count), count)


STEPS = ((0, -1), (0, 1), (-1, -1), (-1, 1), (1, -1), (1, 1))


def dot(a, b):
    return jnp.dot(a, b, preferred_element_type=F32)


def dot_nt(a, b):
    return lax.dot_general(a, b, (((1,), (1,)), ((), ())), preferred_element_type=F32)


def updated(state, moment, grad, entries):
    lane = lax.broadcasted_iota(jnp.int32, (1, LANES), 1)
    squared = jnp.sum(grad * grad, axis=0, keepdims=True)
    one = jnp.sum(jnp.where(lane < SECOND, squared, 0.0), axis=1, keepdims=True) / entries
    two = jnp.sum(jnp.where(lane >= SECOND, squared, 0.0), axis=1, keepdims=True) / entries
    scale = jnp.sqrt(jnp.where(lane < SECOND, one, two) + mean_epsilon)
    moment = momentum_rate * moment + grad / scale
    return state - learn_rate * moment, moment


def rolled(values, shift):
    if shift == 0:
        return values
    return pltpu.roll(values, (-shift) % values.shape[1], axis=1)


def whole_kernel(flat, row_count, col_count, *refs):
    (first_own, first_packed, image, perturb_in, state, moment, pack, unpack, where) = refs[:9]
    (perturb, predict_out, new_state, new_moment) = refs[9:13]
    (
        ext, attacked_cols, slope, hidden, hidden_cols, rest_cols, pre_cols, wide, spread_weight,
        own, packed, target, above, below, beside, target_above, target_below,
        grad, sent, part_rows, half, part_cols, summed,
        rim_sends, rim_recvs, sum_sends, sum_recvs,
    ) = refs[13:]
    C, N, T = flat.channels, flat.total, flat.pitch
    taps = [(a, b) for a in range(3) for b in range(3)]
    K = 9 * C
    low, high = flat.own_low, flat.own_high
    tall = grad.shape[0] // row_count
    levels = [1 << s for s in range(col_count.bit_length() - 1)]
    me_row, me_col = lax.axis_index("rows"), lax.axis_index("cols")

    def exists(down, right):
        return (
            (me_row + down >= 0)
            & (me_row + down < row_count)
            & (me_col + right >= 0)
            & (me_col + right < col_count)
        )

    def partner(level):
        return me_col + level - 2 * level * lax.rem(me_col // level, 2)

    def signal(device):
        pl.semaphore_signal(barrier, inc=1, device_id=device, device_id_type=MESH)

    barrier = pltpu.get_barrier_semaphore()
    greeted = row_count - 1 + len(levels)
    for d in range(1, row_count):
        signal({"rows": position("rows", d), "cols": me_col})
    for level in levels:
        signal({"rows": me_row, "cols": partner(level)})
    for down, right in STEPS:
        there = exists(down, right)
        pl.when(there)(
            functools.partial(signal, {"rows": me_row + down, "cols": me_col + right})
        )
        greeted = greeted + there.astype(jnp.int32)
    pl.semaphore_wait(barrier, greeted)

    def copy_of(source, target, sends, recvs, device):
        return pltpu.make_async_remote_copy(
            src_ref=source,
            dst_ref=target,
            send_sem=sends,
            recv_sem=recvs,
            device_id=device,
            device_id_type=MESH,
        )

    def rim_copies(from_own, from_packed, to_above, to_below, to_beside, k):
        copies = []

        def add(source, target, down, right):
            i = len(copies)
            device = {"rows": me_row + down, "cols": me_col + right}
            copy = copy_of(source, target, rim_sends.at[k, i], rim_recvs.at[k, i], device)
            copies.append((copy, exists(down, right), exists(-down, -right)))

        one, two = flat.lift, flat.lift + flat.edge
        add(from_own.at[:, :, one:two], to_above, 1, 0)
        one, two = flat.down_from, flat.down_from + flat.band
        add(from_own.at[:, :, one:two], to_below, -1, 0)
        if from_packed is not None:
            for j, (down, right) in enumerate(STEPS):
                add(from_packed, to_beside.at[j], -down, -right)
        return copies

    def start(copies):
        for copy, there, _ in copies:
            pl.when(there)(copy.start)

    def finish(copies):
        for copy, there, here in copies:
            pl.when(there)(copy.wait_send)
            pl.when(here)(copy.wait_recv)

    def rim_of(k):
        return rim_copies(own.at[k], packed.at[k], above.at[k], below.at[k], beside.at[k], k)

    own[0] = first_own[0:4]
    packed[0] = first_packed[...]
    begin = rim_of(0)
    start(begin)
    extra = rim_copies(first_own.at[4:5], None, target_above, target_below, None, REPLAYS + 1)
    start(extra)

    row, col = where[0:1, :], where[1:2, :]
    owned = ((row >= 0) & (row < flat.rows) & (col >= 0) & (col < flat.cols)).astype(F32)
    far_row, far_col = row + me_row * flat.rows, col + me_col * flat.cols
    inside = (
        (far_row >= 0)
        & (far_row < flat.rows * row_count)
        & (far_col >= 0)
        & (far_col < flat.cols * col_count)
    ).astype(F32)
    perturb[...] = perturb_in[...]
    new_state[...] = state[...]
    new_moment[...] = moment[...]
    wide[...] = jnp.zeros(wide.shape, BF16)
    own[1:] = jnp.zeros((REPLAYS,) + own.shape[1:], BF16)
    packed[1:] = jnp.zeros((REPLAYS,) + packed.shape[1:], BF16)
    grad[...] = jnp.zeros(grad.shape, F32)
    lane = lax.broadcasted_iota(jnp.int32, (1, LANES), 1)
    has_above, has_below = me_row > 0, me_row < row_count - 1
    end = flat.down_from + flat.lift
    eye = (
        lax.broadcasted_iota(jnp.int32, (LANES, LANES), 0)
        == lax.broadcasted_iota(jnp.int32, (LANES, LANES), 1)
    ).astype(F32).astype(BF16)

    def chosen(packs, height):
        gathered = jnp.zeros((height, LANES), F32)
        for j, ((down, right), from_lane, pairs) in enumerate(flat.places()):
            keep = (lane >= from_lane) & (lane < from_lane + len(pairs)) & exists(down, right)
            gathered = gathered + jnp.where(keep, packs(j).astype(F32), 0.0)
        return gathered.astype(BF16)

    def extend(block, gathered, top, bottom):
        ext[...] = block.astype(F32) + dot(gathered, unpack[...])
        ext[:, 0 : flat.edge] += jnp.where(has_above, top.astype(F32), 0.0)
        ext[:, end:N] += jnp.where(has_below, bottom.astype(F32), 0.0)

    finish(begin)
    finish(extra)
    gathered = chosen(lambda j: beside[0, j, 4 * C : 5 * C], C)
    extend(first_own[4], gathered, target_above[0], target_below[0])
    target[...] = ext[...]

    def sum_copies(k):
        rows_out = []
        for d in range(1, row_count):
            there = position("rows", d)
            rows_out.append(
                copy_of(
                    sent.at[k, pl.ds(there * tall, tall)],
                    part_rows.at[k, d - 1],
                    sum_sends.at[k, d - 1],
                    sum_recvs.at[k, d - 1],
                    {"rows": there, "cols": me_col},
                )
            )
        cols_out = []
        for i, level in enumerate(levels):
            at = row_count - 1 + i
            cols_out.append(
                copy_of(
                    half.at[k, i],
                    part_cols.at[k, i],
                    sum_sends.at[k, at],
                    sum_recvs.at[k, at],
                    {"rows": me_row, "cols": partner(level)},
                )
            )
        band = pl.ds(me_row * tall, tall)
        back_out = []
        for d in range(1, row_count):
            at = row_count - 2 + len(levels) + d
            back_out.append(
                copy_of(
                    summed.at[k, band],
                    summed.at[k, band],
                    sum_sends.at[k, at],
                    sum_recvs.at[k, at],
                    {"rows": position("rows", d), "cols": me_col},
                )
            )
        return rows_out, cols_out, back_out

    def replay(k):
        fast = new_state[...].astype(BF16)
        ahead = dot_nt(eye, fast).astype(BF16)
        ahead_one, ahead_two = ahead[0:C, :], ahead[SECOND : SECOND + C, :]
        from_lane = lax.broadcasted_iota(jnp.int32, (LANES, K), 0)
        to_lane = lax.broadcasted_iota(jnp.int32, (LANES, K), 1)
        back_one = jnp.zeros((C, K), F32)
        for i in range(9):
            put = ((to_lane == from_lane + i * C) & (from_lane < C)).astype(F32).astype(BF16)
            back_one = back_one + dot(fast[i * C : (i + 1) * C, :], put)
        back_one = back_one.astype(BF16)
        four = 4 * C
        from_lane = lax.broadcasted_iota(jnp.int32, (LANES, four), 0)
        to_lane = lax.broadcasted_iota(jnp.int32, (LANES, four), 1)
        for py in range(2):
            for px in range(2):
                block = jnp.zeros((C, four), F32)
                for a, dy in ([(1, 0)] if py == 0 else [(0, 1), (2, 0)]):
                    for b, dx in ([(1, 0)] if px == 0 else [(0, 1), (2, 0)]):
                        i = 3 * a + b
                        slot = 2 * dy + dx
                        put = (
                            (to_lane == from_lane - SECOND + slot * C)
                            & (from_lane >= SECOND)
                            & (from_lane < SECOND + C)
                        ).astype(F32).astype(BF16)
                        block = block + dot(fast[i * C : (i + 1) * C, :], put)
                spread_weight[(2 * py + px) * C : (2 * py + px + 1) * C, :] = block.astype(BF16)

        gathered = chosen(lambda j: beside[k, j, 0 : 4 * C], 4 * C)
        for p in range(4):
            extend(own[k, p], gathered[p * C : (p + 1) * C, :], above[k, p], below[k, p])
            full = ext[...]
            for i, (a, b) in enumerate(taps):
                moved = rolled(full, (a - 1) * T + (b - 1))
                attacked_cols[p, i * C : (i + 1) * C, :] = moved.astype(BF16)
            pre_value = dot(ahead_one, attacked_cols[p])
            sigmoid_value = jax.nn.sigmoid(pre_value)
            hidden[p] = pre_value * sigmoid_value * inside
            slope[p] = sigmoid_value * (1.0 + pre_value * (1.0 - sigmoid_value)) * inside
        for i, (a, b) in enumerate(taps):
            py, dy = [(1, -1), (0, 0), (1, 0)][a]
            px, dx = [(1, -1), (0, 0), (1, 0)][b]
            moved = rolled(hidden[2 * py + px], dy * T + dx)
            hidden_cols[i * C : (i + 1) * C, :] = moved.astype(BF16)
        predict = dot(ahead_two, hidden_cols[...])
        predict_out[...] = predict.astype(BF16)
        residual = (predict - target[...]) * inside
        wide[0:C, :] = jnp.zeros((C, high - low), BF16)
        wide[SECOND : SECOND + C, :] = (residual * owned)[:, low:high].astype(BF16)
        total = dot_nt(hidden_cols[:, low:high], wide[...])
        wide[SECOND : SECOND + C, :] = jnp.zeros((C, high - low), BF16)
        for i, shift in enumerate((0, 1, T, T + 1)):
            rest_cols[i * C : (i + 1) * C, :] = rolled(residual, shift).astype(BF16)
        hidden_grad = dot(spread_weight[...], rest_cols[...])
        for p in range(4):
            pre_grad = hidden_grad[p * C : (p + 1) * C, :] * slope[p]
            hidden[p] = pre_grad
            wide[0:C, :] = (pre_grad * owned)[:, low:high].astype(BF16)
            total = total + dot_nt(attacked_cols[p, :, low:high], wide[...])
        grad[0:K, :] = total
        sent[k] = grad[...].astype(BF16)
        rows_out, cols_out, back_out = sum_copies(k)
        for copy in rows_out:
            copy.start()

        def input_side(p):
            pre_grad = hidden[p]
            for i, (a, b) in enumerate(taps):
                moved = rolled(pre_grad, -((a - 1) * T + (b - 1)))
                pre_cols[i * C : (i + 1) * C, :] = moved[:, low:high].astype(BF16)
            input_grad = dot(back_one, pre_cols[...])
            moved = jnp.clip(
                perturb[p, :, low:high] + step_size * jnp.tanh(input_grad), -clip_bound, clip_bound
            )
            moved = moved * owned[:, low:high]
            perturb[p, :, low:high] = moved
            attacked = (image[p, :, low:high].astype(F32) + moved).astype(BF16)
            own[k + 1, p, :, low:high] = attacked
            packed[k + 1, p * C : (p + 1) * C, :] = dot(attacked, pack[low:high, :]).astype(BF16)

        input_side(0)
        for copy in rows_out:
            copy.wait()
        part = grad[pl.ds(pl.multiple_of(me_row * tall, 8), tall)]
        for d in range(1, row_count):
            part = part + part_rows[k, d - 1].astype(F32)
        for i in range(len(levels)):
            half[k, i] = part.astype(BF16)
            cols_out[i].start()
            if i < 2:
                input_side(i + 1)
            if i == 1:
                input_side(3)
                following = rim_of(k + 1)
                start(following)
            cols_out[i].wait()
            part = half[k, i].astype(F32) + part_cols[k, i].astype(F32)
        summed[k, pl.ds(pl.multiple_of(me_row * tall, 16), tall)] = part.astype(BF16)
        for copy in back_out:
            copy.start()
        for copy in back_out:
            copy.wait()
        now, later = updated(
            new_state[...], new_moment[...], summed[k, 0:K, :].astype(F32), K * C
        )
        new_state[...] = now
        new_moment[...] = later
        finish(following)

    @pl.loop(0, REPLAYS)
    def _(k):
        replay(k)


def whole(flat, tables, own, packed, image, perturb, state, moment, tall):
    C, N = flat.channels, flat.total
    K = 9 * C
    row_count, col_count = lax.axis_size("rows"), lax.axis_size("cols")
    levels = col_count.bit_length() - 1
    width = flat.own_high - flat.own_low
    short = tall // row_count
    operands = [own, packed, image, perturb, state, moment, *tables]
    shapes = [
        jax.ShapeDtypeStruct((4, C, N), F32),
        jax.ShapeDtypeStruct((C, N), BF16),
        jax.ShapeDtypeStruct((K, LANES), F32),
        jax.ShapeDtypeStruct((K, LANES), F32),
    ]
    slots = REPLAYS + 1
    sums = 2 * (row_count - 1) + levels
    scratch = [
        pltpu.VMEM((C, N), F32),
        pltpu.VMEM((4, K, N), BF16),
        pltpu.VMEM((4, C, N), F32),
        pltpu.VMEM((4, C, N), F32),
        pltpu.VMEM((K, N), BF16),
        pltpu.VMEM((4 * C, N), BF16),
        pltpu.VMEM((K, width), BF16),
        pltpu.VMEM((LANES, width), BF16),
        pltpu.VMEM((4 * C, 4 * C), BF16),
        pltpu.VMEM((slots, 4, C, N), BF16),
        pltpu.VMEM((slots, 5 * C, LANES), BF16),
        pltpu.VMEM((C, N), F32),
        pltpu.VMEM((slots, 4, C, flat.edge), BF16),
        pltpu.VMEM((slots, 4, C, flat.band), BF16),
        pltpu.VMEM((slots, len(STEPS), 5 * C, LANES), BF16),
        pltpu.VMEM((1, C, flat.edge), BF16),
        pltpu.VMEM((1, C, flat.band), BF16),
        pltpu.VMEM((tall, LANES), F32),
        pltpu.VMEM((REPLAYS, tall, LANES), BF16),
        pltpu.VMEM((REPLAYS, row_count - 1, short, LANES), BF16),
        pltpu.VMEM((REPLAYS, levels, short, LANES), BF16),
        pltpu.VMEM((REPLAYS, levels, short, LANES), BF16),
        pltpu.VMEM((REPLAYS, tall, LANES), BF16),
        pltpu.SemaphoreType.DMA((slots + 1, 8)),
        pltpu.SemaphoreType.DMA((slots + 1, 8)),
        pltpu.SemaphoreType.DMA((REPLAYS, sums)),
        pltpu.SemaphoreType.DMA((REPLAYS, sums)),
    ]
    return pl.pallas_call(
        functools.partial(whole_kernel, flat, row_count, col_count),
        out_shape=shapes,
        in_specs=[WHOLE] * len(operands),
        out_specs=[WHOLE] * len(shapes),
        scratch_shapes=scratch,
        compiler_params=pltpu.CompilerParams(
            collective_id=0, has_side_effects=True, vmem_limit_bytes=VMEM_LIMIT
        ),
    )(*operands)


def parted(flat, block):
    C, h, w = flat.channels, flat.rows, flat.cols
    order = np.zeros((2 * w, 2 * w), np.float32)
    for c in range(w):
        order[2 * c, c] = 1
        order[2 * c + 1, w + c] = 1
    order = jnp.asarray(order, block.dtype)
    sorted_cols = jnp.dot(
        block.reshape(C * 2 * h, 2 * w),
        order,
        precision=lax.Precision.HIGHEST if block.dtype == F32 else None,
        preferred_element_type=block.dtype,
    )
    planes = sorted_cols.reshape(C, h, 2, 2, w).transpose(2, 3, 0, 1, 4).reshape(4, C, h, w)
    return laid(flat, planes)


def laid(flat, planes):
    count = planes.shape[0]
    right = flat.pitch - flat.cols - RIM
    planes = jnp.pad(planes, ((0, 0), (0, 0), (RIM, RIM), (RIM, right)))
    planes = planes.reshape(count, flat.channels, -1)
    return jnp.pad(planes, ((0, 0), (0, 0), (0, flat.total - planes.shape[2])))


def unlaid(flat, planes):
    count = planes.shape[0]
    planes = planes[:, :, : (flat.rows + 2 * RIM) * flat.pitch]
    planes = planes.reshape(count, flat.channels, flat.rows + 2 * RIM, flat.pitch)
    return planes[:, :, RIM : RIM + flat.rows, RIM : RIM + flat.cols]


def joined(flat, planes):
    C, h, w = flat.channels, flat.rows, flat.cols
    order = np.zeros((2 * w, 2 * w), np.float32)
    for c in range(w):
        order[c, 2 * c] = 1
        order[w + c, 2 * c + 1] = 1
    blocks = unlaid(flat, planes).reshape(2, 2, C, h, w).transpose(2, 3, 0, 1, 4)
    blocks = jnp.dot(
        blocks.reshape(C * 2 * h, 2 * w), jnp.asarray(order), precision=lax.Precision.HIGHEST
    )
    return blocks.reshape(C, 2 * h, 2 * w)


def stacked(one, two):
    C = one.shape[0]
    one, two = (k.transpose(2, 3, 1, 0).reshape(9 * C, C) for k in (one, two))
    one = jnp.pad(one, ((0, 0), (0, SECOND - C)))
    two = jnp.pad(two, ((0, 0), (0, SECOND - C)))
    return jnp.concatenate([one, two], axis=1)


def unstacked(both, C):
    return tuple(
        both[:, low : low + C].reshape(3, 3, C, C).transpose(3, 2, 0, 1) for low in (0, SECOND)
    )


def body(image, perturb, target, kernel_one, kernel_two, moment_one, moment_two):
    C = image.shape[0]
    flat = Flat(C, target.shape[1], target.shape[2])
    tables = tuple(jnp.asarray(t) for t in flat.tables())
    pieces = 16 * lax.axis_size("rows")
    tall = -(-9 * C // pieces) * pieces
    image = parted(flat, image)
    perturb = parted(flat, perturb)
    state = stacked(kernel_one, kernel_two)
    moment = stacked(moment_one, moment_two)
    own = (image.astype(F32) + perturb).astype(BF16)
    own = jnp.concatenate([own, laid(flat, target[None])], axis=0)
    packed = jnp.dot(
        own.reshape(5 * C, flat.total), tables[0], preferred_element_type=F32
    ).astype(BF16)
    perturb, predict, state, moment = whole(
        flat, tables, own, packed, image, perturb, state, moment, tall
    )
    new_one, new_two = unstacked(state, C)
    new_moment_one, new_moment_two = unstacked(moment, C)
    prediction = unlaid(flat, predict[None])[0]
    return (joined(flat, perturb), prediction, new_one, new_two, new_moment_one, new_moment_two)


def solution(mesh):
    in_specs = (
        P(None, "rows", "cols"),
        P(None, "rows", "cols"),
        P(None, "rows", "cols"),
        P(),
        P(),
        P(),
        P(),
    )
    out_specs = (P(None, "rows", "cols"), P(None, "rows", "cols"), P(), P(), P(), P())
    return jax.shard_map(body, mesh=mesh, in_specs=in_specs, out_specs=out_specs, check_vma=False)
```

time: 792 us -> 122 us (0.15); the launches traced: 782 us -> 122 us
  waiting for transfers between devices: 377 us -> 0 us
  local copies, waits for them, and re-layouts: 163 us -> 23.4 us
  starting transfers between devices: 96.1 us -> 0 us
  Pallas kernels: 0 us -> 87.9 us
  matrix products: 89.8 us -> 4.73 us
  other arithmetic: 35.4 us -> 4.88 us
  between operations: 20.5 us -> 0.86 us
    psum x3 -> x0, waiting for transfers between devices: 348 us -> none  [body(): grad_one = lax.psum(grad_one, ('rows', 'cols'))]
    ppermute x36 -> x0, starting transfers between devices: 95.4 us -> none  [the longest x12 49.5 us: with_halo(): lax.ppermute(lax.slice_in_dim(block, block.shape[dim] - width, None, axis...]
    pallas_call x0 -> x1, Pallas kernels: none -> 87.9 us  [whole(): pl.pallas_call(functools.partial(whole_kernel, flat, row_count, col_count...]
    transpose x6 -> x0, matrix products: 62.4 us -> none  [kernel_grad(): return jnp.transpose(summed, (1, 0, 2, 3))]
    conv_general_dilated x42 -> x0, local copies, waits for them, and re-layouts: 57.2 us -> none  [the longest x33 54.5 us: plain_conv(): lax.conv_general_dilated(source[None], kernel, (stride, stride), 'VALID',...]
    broadcast_in_dim x18 -> x0, local copies, waits for them, and re-layouts: 32.2 us -> none  [the longest x15 32 us: plain_conv(): source[None]]
    ppermute x36 -> x0, waiting for transfers between devices: 29 us -> none  [the longest x12 18.7 us: with_halo(): lax.ppermute(lax.slice_in_dim(block, block.shape[dim] - width, None, axis...]
    conv_general_dilated x12 -> x0, matrix products: 27.4 us -> none  [the longest x9 23.4 us: plain_conv(): lax.conv_general_dilated(source[None], kernel, (stride, stride), 'VALID',...]
  transfers between devices with their start and end apart: 39 -> 0, of which waited for: 14 -> 0; matrix products, arithmetic and copies ran while one was open for 20% -> 0% of each run, Pallas kernels for 0% -> 0%
where the time goes in v2:
time: 122 us
  Pallas kernels  87.9 us (72%)
  local copies, waits for them, and re-layouts  23.4 us (19%)
  other arithmetic  4.88 us (4%)
  matrix products  4.73 us (4%)
    pallas_call x1, Pallas kernels, whole(): pl.pallas_call(functools.partial(whole_kernel, flat, row_count, col_count...  87.9 us
    reshape x3, local copies, waits for them, and re-layouts, laid(): planes = planes.reshape(count, flat.channels, -1)  6.42 us
    reshape x2, local copies, waits for them, and re-layouts, unlaid(): planes.reshape(count, flat.channels, flat.rows + 2 * RIM, flat.pitch)  4.1 us
    reshape x4, local copies, waits for them, and re-layouts, unstacked(): both[:, low:low + C].reshape(3, 3, C, C).transpose(3, 2, 0, 1)  3.26 us
    pad x1, other arithmetic, laid(): return jnp.pad(planes, ((0, 0), (0, 0), (0, flat.total - planes.shape[2])))  3.15 us

profile of v2, /device:TPU:0, one launch (start us, length us, event | category | flops | bytes accessed | tf_op | source)
XLA Modules:
  0.0 121.7 jit_solution(9288288227077299063)
XLA Ops:
  0.6 1.1 copy.45
  1.7 1.2 convolution_bitcast_fusion.1
  3.1 0.8 pad.37
  4.0 3.0 %reshape.78 = bf16[4,48,2016]{2,1,0:T(8,128)(2,1)} reshape(bf16[4,48,14,144]{3,2,1,0:T(8,128)(2,1)S(1)} %pad.37) | data formatting | bytes 1548288 | tf_op jit(solution)/shard_map/reshape | solution.py:472
  7.5 0.8 convolution_bitcast_fusion
  8.8 0.9 pad.39
  9.7 2.9 %reshape.80 = f32[4,48,2016]{2,1,0:T(8,128)} reshape(f32[4,48,14,144]{3,2,1,0:T(8,128)S(1)} %pad.39) | data formatting | bytes 3096576 | tf_op jit(solution)/shard_map/reshape | solution.py:472
  12.6 3.1 %fusion.2 = (f32[4,48,2048]{2,1,0:T(8,128)}, bf16[4,48,2048]{2,1,0:T(8,128)(2,1)S(1)}) fusion(f32[4,48,2016]{2,1,0:T(8,128)} %reshape.80, bf16[4,48,2016]{2,1,0:T(8,128)(2,1)} %reshape.78), kind=kLoop, calls=%fused_computation.13 | loop fusion | flops 1179648 | bytes 4681728 | tf_op jit(solution)/shard_map/jit(_pad)/pad | solution.py:473
  16.8 1.0 convolution_convert_fusion.refs_1_
  17.9 0.9 pad.38.refs_2_
  19.1 0.8 select_maximum_fusion.refs_5_
  20.2 0.8 select_maximum_fusion.1.refs_4_
  21.0 87.9 %shard_map.172 = (f32[4,48,2048]{2,1,0:T(8,128)}, bf16[48,2048]{1,0:T(8,128)(2,1)}, f32[432,128]{1,0:T(8,128)}, f32[432,128]{1,0:T(8,128)}) custom-call(bf16[5,48,2048]{2,1,0:T(8,128)(2,1)} %copy-done, bf16[240,128]{1,0:T(8,128)(2,1)} %convolution_convert_fusion.refs_1_, bf16[4,48,2048]{2,1,0:T(8,128)(2,1)} %pad.38.refs_2_, ...), custom_call_target="tpu_custom_call" | custom-call | tf_op jit(solution)/shard_map/pallas_call | solution.py:439
  108.9 1.4 %fusion.3 = (f32[432,48]{1,0:T(8,128)S(1)}, f32[432,48]{1,0:T(8,128)S(1)}, f32[432,48]{1,0:T(8,128)S(1)}, f32[432,48]{1,0:T(8,128)S(1)}) fusion(f32[432,128]{1,0:T(8,128)} %get-tuple-element.13, f32[432,128]{1,0:T(8,128)} %get-tuple-element.12), kind=kLoop, calls=%fused_computation.14 | loop fusion | bytes 663552 | tf_op jit(solution)/shard_map/slice | solution.py:506
  110.3 0.8 copy.39
  111.2 0.8 copy.40
  112.0 0.8 copy.41
  112.8 0.8 copy.42
  113.6 3.5 %reshape.87 = f32[4,48,14,144]{3,2,1,0:T(8,128)S(1)} reshape(f32[4,48,2016]{2,1,0:T(8,128)} %bitcast.61) | data formatting | bytes 3096576 | tf_op jit(solution)/shard_map/reshape | solution.py:479
  117.4 0.6 copy.48
  118.1 0.6 dot_general.35
  118.7 1.7 %fusion.5 = f32[48,16,256]{2,1,0:T(8,128)} fusion(f32[48,16,256]{2,1,0:T(8,128)S(1)} %dot_general.35, f32[256,256,1]{1,0,2:T(8,128)S(1)} %copy-done.4), kind=kOutput, calls=%fused_computation.16 | convolution fusion | flops 603979776 | bytes 1835008 | tf_op jit(solution)/shard_map/dot_general | solution.py:490
  120.4 0.6 reshape.89
  121.0 0.8 slice_bitcast_fusion
  (35 shorter events, 2.9 us)
Async XLA Ops:
  4.0 3.0 %copy-start.3 = (f32[48,16,256]{2,1,0:T(8,128)S(1)}, f32[48,16,256]{2,1,0:T(8,128)}, u32[]{:S(2)}) copy-start(f32[48,16,256]{2,1,0:T(8,128)} %param.14) | copy-start | bytes 2359300
  4.0 3.5 %copy-start.5 = (f32[2,128,256,1,1]{2,1,4,3,0:T(8,128)S(1)}, f32[2,128,256,1,1]{2,1,4,3,0:T(8,128)}, u32[]{:S(2)}) copy-start(f32[2,128,256,1,1]{2,1,4,3,0:T(8,128)} %constant.48) | copy-start | bytes 786436
  12.6 3.2 %copy-start.11 = (bf16[48,8,128]{2,1,0:T(8,128)(2,1)S(1)}, bf16[48,8,128]{2,1,0:T(8,128)(2,1)}, u32[]{:S(2)}) copy-start(bf16[48,8,128]{2,1,0:T(8,128)(2,1)} %param.15) | copy-start | bytes 294916
  15.7 1.0 copy-start.2
  16.4 1.4 %copy-start.1 = (bf16[4,48,2016]{2,1,0:T(8,128)(2,1)S(1)}, bf16[4,48,2016]{2,1,0:T(8,128)(2,1)}, u32[]{:S(2)}) copy-start(bf16[4,48,2016]{2,1,0:T(8,128)(2,1)} %reshape.78) | copy-start | bytes 2322436
  16.6 2.3 %copy-start = (bf16[5,48,2048]{2,1,0:T(8,128)(2,1)}, bf16[5,48,2048]{2,1,0:T(8,128)(2,1)S(1)}, u32[]{:S(2)}) copy-start(bf16[5,48,2048]{2,1,0:T(8,128)(2,1)S(1)} %fusion.1.refs_0_) | copy-start | bytes 2949124
  16.8 2.0 %copy-start.6 = (f32[48,48,3,3]{1,0,3,2:T(8,128)S(1)}, f32[48,48,3,3]{1,0,3,2:T(8,128)}, u32[]{:S(2)}) copy-start(f32[48,48,3,3]{1,0,3,2:T(8,128)} %param.18) | copy-start | bytes 248836
  16.8 2.2 %copy-start.7 = (f32[48,48,3,3]{1,0,3,2:T(8,128)S(1)}, f32[48,48,3,3]{1,0,3,2:T(8,128)}, u32[]{:S(2)}) copy-start(f32[48,48,3,3]{1,0,3,2:T(8,128)} %param.19) | copy-start | bytes 248836
  17.8 2.1 %copy-start.8 = (f32[48,48,3,3]{1,0,3,2:T(8,128)S(1)}, f32[48,48,3,3]{1,0,3,2:T(8,128)}, u32[]{:S(2)}) copy-start(f32[48,48,3,3]{1,0,3,2:T(8,128)} %param.16) | copy-start | bytes 248836
  17.9 2.2 %copy-start.9 = (f32[48,48,3,3]{1,0,3,2:T(8,128)S(1)}, f32[48,48,3,3]{1,0,3,2:T(8,128)}, u32[]{:S(2)}) copy-start(f32[48,48,3,3]{1,0,3,2:T(8,128)} %param.17) | copy-start | bytes 248836
  117.4 1.3 %copy-start.4 = (f32[256,256,1]{1,0,2:T(8,128)S(1)}, f32[256,256,1]{1,0,2:T(8,128)}, u32[]{:S(2)}) copy-start(f32[256,256,1]{1,0,2:T(8,128)} %constant.49) | copy-start | bytes 786436
  118.1 2.3 %copy-start.10 = (bf16[48,2048]{1,0:T(8,128)(2,1)S(1)}, bf16[48,2048]{1,0:T(8,128)(2,1)}, u32[]{:S(2)}) copy-start(bf16[48,2048]{1,0:T(8,128)(2,1)} %get-tuple-element.11) | copy-start | bytes 589828

commit v3 on v2

--- a/solution.py
+++ b/solution.py
@@ -103,14 +103,15 @@
 
 
 def whole_kernel(flat, row_count, col_count, *refs):
-    (first_own, first_packed, image, perturb_in, state, moment, pack, unpack, where) = refs[:9]
-    (perturb, predict_out, new_state, new_moment) = refs[9:13]
+    (image_in, perturb_in, target_in, state, moment, pack, unpack, where) = refs[:8]
+    (perturb_out, predict_out, new_state, new_moment) = refs[8:12]
     (
         ext, attacked_cols, slope, hidden, hidden_cols, rest_cols, pre_cols, wide, spread_weight,
         own, packed, target, above, below, beside, target_above, target_below,
         grad, sent, part_rows, half, part_cols, summed,
         rim_sends, rim_recvs, sum_sends, sum_recvs,
-    ) = refs[13:]
+            image, perturb, target_own,
+    ) = refs[12:]
     C, N, T = flat.channels, flat.total, flat.pitch
     taps = [(a, b) for a in range(3) for b in range(3)]
     K = 9 * C
@@ -145,6 +146,40 @@
             functools.partial(signal, {"rows": me_row + down, "cols": me_col + right})
         )
         greeted = greeted + there.astype(jnp.int32)
+
+    row, col = where[0:1, :], where[1:2, :]
+    owned = ((row >= 0) & (row < flat.rows) & (col >= 0) & (col < flat.cols)).astype(F32)
+    w = flat.cols
+    from_col = lax.broadcasted_iota(jnp.int32, (2 * w, 2 * w), 0)
+    to_col = lax.broadcasted_iota(jnp.int32, (2 * w, 2 * w), 1)
+    sorted_from = jnp.where(to_col < w, 2 * to_col, 2 * (to_col - w) + 1)
+    order = (from_col == sorted_from).astype(F32)
+    own[1:] = jnp.zeros((REPLAYS,) + own.shape[1:], BF16)
+    packed[1:] = jnp.zeros((REPLAYS,) + packed.shape[1:], BF16)
+    ext[...] = jnp.zeros(ext.shape, F32)
+    perturb[...] = jnp.zeros(perturb.shape, F32)
+    hidden[...] = jnp.zeros(hidden.shape, F32)
+    for r in range(flat.rows):
+        spot = flat.at(r, 0)
+        ext[:, spot : spot + w] = target_in[r].astype(F32)
+        for py in range(2):
+            parts = dot(image_in[2 * r + py], order.astype(BF16))
+            hidden[2 * py, :, spot : spot + w] = parts[:, :w]
+            hidden[2 * py + 1, :, spot : spot + w] = parts[:, w:]
+            parts = jnp.dot(
+                perturb_in[2 * r + py],
+                order,
+                precision=lax.Precision.HIGHEST,
+                preferred_element_type=F32,
+            )
+            perturb[2 * py, :, spot : spot + w] = parts[:, :w]
+            perturb[2 * py + 1, :, spot : spot + w] = parts[:, w:]
+    target_own[0] = ext[...].astype(BF16)
+    packed[0, 4 * C : 5 * C, :] = dot(target_own[0], pack[...]).astype(BF16)
+    for p in range(4):
+        image[p] = hidden[p].astype(BF16)
+        own[0, p] = (hidden[p] + perturb[p]).astype(BF16)
+        packed[0, p * C : (p + 1) * C, :] = dot(own[0, p], pack[...]).astype(BF16)
     pl.semaphore_wait(barrier, greeted)
 
     def copy_of(source, target, sends, recvs, device):
@@ -187,15 +222,11 @@
     def rim_of(k):
         return rim_copies(own.at[k], packed.at[k], above.at[k], below.at[k], beside.at[k], k)
 
-    own[0] = first_own[0:4]
-    packed[0] = first_packed[...]
     begin = rim_of(0)
     start(begin)
-    extra = rim_copies(first_own.at[4:5], None, target_above, target_below, None, REPLAYS + 1)
+    extra = rim_copies(target_own, None, target_above, target_below, None, REPLAYS + 1)
     start(extra)
 
-    row, col = where[0:1, :], where[1:2, :]
-    owned = ((row >= 0) & (row < flat.rows) & (col >= 0) & (col < flat.cols)).astype(F32)
     far_row, far_col = row + me_row * flat.rows, col + me_col * flat.cols
     inside = (
         (far_row >= 0)
@@ -203,12 +234,9 @@
         & (far_col >= 0)
         & (far_col < flat.cols * col_count)
     ).astype(F32)
-    perturb[...] = perturb_in[...]
     new_state[...] = state[...]
     new_moment[...] = moment[...]
     wide[...] = jnp.zeros(wide.shape, BF16)
-    own[1:] = jnp.zeros((REPLAYS,) + own.shape[1:], BF16)
-    packed[1:] = jnp.zeros((REPLAYS,) + packed.shape[1:], BF16)
     grad[...] = jnp.zeros(grad.shape, F32)
     lane = lax.broadcasted_iota(jnp.int32, (1, LANES), 1)
     has_above, has_below = me_row > 0, me_row < row_count - 1
@@ -233,7 +261,7 @@
     finish(begin)
     finish(extra)
     gathered = chosen(lambda j: beside[0, j, 4 * C : 5 * C], C)
-    extend(first_own[4], gathered, target_above[0], target_below[0])
+    extend(target_own[0], gathered, target_above[0], target_below[0])
     target[...] = ext[...]
 
     def sum_copies(k):
@@ -322,7 +350,7 @@
             moved = rolled(hidden[2 * py + px], dy * T + dx)
             hidden_cols[i * C : (i + 1) * C, :] = moved.astype(BF16)
         predict = dot(ahead_two, hidden_cols[...])
-        predict_out[...] = predict.astype(BF16)
+        ext[...] = predict
         residual = (predict - target[...]) * inside
         wide[0:C, :] = jnp.zeros((C, high - low), BF16)
         wide[SECOND : SECOND + C, :] = (residual * owned)[:, low:high].astype(BF16)
@@ -390,18 +418,33 @@
     def _(k):
         replay(k)
 
-
-def whole(flat, tables, own, packed, image, perturb, state, moment, tall):
+    for r in range(flat.rows):
+        spot = flat.at(r, 0)
+        predict_out[r] = ext[:, spot : spot + w].astype(BF16)
+        for py in range(2):
+            parts = jnp.concatenate(
+                [perturb[2 * py, :, spot : spot + w], perturb[2 * py + 1, :, spot : spot + w]], axis=1
+            )
+            perturb_out[2 * r + py] = lax.dot_general(
+                parts,
+                order,
+                (((1,), (1,)), ((), ())),
+                precision=lax.Precision.HIGHEST,
+                preferred_element_type=F32,
+            )
+
+
+def whole(flat, tables, image, perturb, target, state, moment, tall):
     C, N = flat.channels, flat.total
     K = 9 * C
     row_count, col_count = lax.axis_size("rows"), lax.axis_size("cols")
     levels = col_count.bit_length() - 1
     width = flat.own_high - flat.own_low
     short = tall // row_count
-    operands = [own, packed, image, perturb, state, moment, *tables]
+    operands = [image, perturb, target, state, moment, *tables]
     shapes = [
-        jax.ShapeDtypeStruct((4, C, N), F32),
-        jax.ShapeDtypeStruct((C, N), BF16),
+        jax.ShapeDtypeStruct(perturb.shape, F32),
+        jax.ShapeDtypeStruct(target.shape, BF16),
         jax.ShapeDtypeStruct((K, LANES), F32),
         jax.ShapeDtypeStruct((K, LANES), F32),
     ]
@@ -435,6 +478,9 @@
         pltpu.SemaphoreType.DMA((slots + 1, 8)),
         pltpu.SemaphoreType.DMA((REPLAYS, sums)),
         pltpu.SemaphoreType.DMA((REPLAYS, sums)),
+        pltpu.VMEM((4, C, N), BF16),
+        pltpu.VMEM((4, C, N), F32),
+        pltpu.VMEM((1, C, N), BF16),
     ]
     return pl.pallas_call(
         functools.partial(whole_kernel, flat, row_count, col_count),
@@ -448,51 +494,6 @@
     )(*operands)
 
 
-def parted(flat, block):
-    C, h, w = flat.channels, flat.rows, flat.cols
-    order = np.zeros((2 * w, 2 * w), np.float32)
-    for c in range(w):
-        order[2 * c, c] = 1
-        order[2 * c + 1, w + c] = 1
-    order = jnp.asarray(order, block.dtype)
-    sorted_cols = jnp.dot(
-        block.reshape(C * 2 * h, 2 * w),
-        order,
-        precision=lax.Precision.HIGHEST if block.dtype == F32 else None,
-        preferred_element_type=block.dtype,
-    )
-    planes = sorted_cols.reshape(C, h, 2, 2, w).transpose(2, 3, 0, 1, 4).reshape(4, C, h, w)
-    return laid(flat, planes)
-
-
-def laid(flat, planes):
-    count = planes.shape[0]
-    right = flat.pitch - flat.cols - RIM
-    planes = jnp.pad(planes, ((0, 0), (0, 0), (RIM, RIM), (RIM, right)))
-    planes = planes.reshape(count, flat.channels, -1)
-    return jnp.pad(planes, ((0, 0), (0, 0), (0, flat.total - planes.shape[2])))
-
-
-def unlaid(flat, planes):
-    count = planes.shape[0]
-    planes = planes[:, :, : (flat.rows + 2 * RIM) * flat.pitch]
-    planes = planes.reshape(count, flat.channels, flat.rows + 2 * RIM, flat.pitch)
-    return planes[:, :, RIM : RIM + flat.rows, RIM : RIM + flat.cols]
-
-
-def joined(flat, planes):
-    C, h, w = flat.channels, flat.rows, flat.cols
-    order = np.zeros((2 * w, 2 * w), np.float32)
-    for c in range(w):
-        order[c, 2 * c] = 1
-        order[w + c, 2 * c + 1] = 1
-    blocks = unlaid(flat, planes).reshape(2, 2, C, h, w).transpose(2, 3, 0, 1, 4)
-    blocks = jnp.dot(
-        blocks.reshape(C * 2 * h, 2 * w), jnp.asarray(order), precision=lax.Precision.HIGHEST
-    )
-    return blocks.reshape(C, 2 * h, 2 * w)
-
-
 def stacked(one, two):
     C = one.shape[0]
     one, two = (k.transpose(2, 3, 1, 0).reshape(9 * C, C) for k in (one, two))
@@ -513,22 +514,16 @@
     tables = tuple(jnp.asarray(t) for t in flat.tables())
     pieces = 16 * lax.axis_size("rows")
     tall = -(-9 * C // pieces) * pieces
-    image = parted(flat, image)
-    perturb = parted(flat, perturb)
     state = stacked(kernel_one, kernel_two)
     moment = stacked(moment_one, moment_two)
-    own = (image.astype(F32) + perturb).astype(BF16)
-    own = jnp.concatenate([own, laid(flat, target[None])], axis=0)
-    packed = jnp.dot(
-        own.reshape(5 * C, flat.total), tables[0], preferred_element_type=F32
-    ).astype(BF16)
+    image, perturb, target = (x.transpose(1, 0, 2) for x in (image, perturb, target))
     perturb, predict, state, moment = whole(
-        flat, tables, own, packed, image, perturb, state, moment, tall
+        flat, tables, image, perturb, target, state, moment, tall
     )
     new_one, new_two = unstacked(state, C)
     new_moment_one, new_moment_two = unstacked(moment, C)
-    prediction = unlaid(flat, predict[None])[0]
-    return (joined(flat, perturb), prediction, new_one, new_two, new_moment_one, new_moment_two)
+    perturb, prediction = perturb.transpose(1, 0, 2), predict.transpose(1, 0, 2)
+    return (perturb, prediction, new_one, new_two, new_moment_one, new_moment_two)
 
 
 def solution(mesh):

time: 122 us -> 104 us (0.85)
  local copies, waits for them, and re-layouts: 23.4 us -> 12.9 us
  matrix products: 4.73 us -> 0 us
  other arithmetic: 4.88 us -> 1.63 us
    reshape x6 -> x0, local copies, waits for them, and re-layouts: 11.1 us -> none  [the longest x3 6.42 us: laid(): planes = planes.reshape(count, flat.channels, -1)]
    unnamed x24 -> x21, local copies, waits for them, and re-layouts: 0.33 us -> 7.96 us
    dot_general x4 -> x0, matrix products: 4.73 us -> none  [the longest x2 2.03 us: parted(): jnp.dot(block.reshape(C * 2 * h, 2 * w), order, precision=lax.Precision.H...]
    pad x1 -> x0, other arithmetic: 3.15 us -> none  [laid(): return jnp.pad(planes, ((0, 0), (0, 0), (0, flat.total - planes.shape[2])))]
    pad x4 -> x0, local copies, waits for them, and re-layouts: 2.86 us -> none  [the longest x3 1.92 us: laid(): planes = jnp.pad(planes, ((0, 0), (0, 0), (RIM, RIM), (RIM, right)))]
    dot_general x3 -> x0, local copies, waits for them, and re-layouts: 2.2 us -> none  [the longest x2 1.57 us: parted(): jnp.dot(block.reshape(C * 2 * h, 2 * w), order, precision=lax.Precision.H...]
    slice x1, local copies, waits for them, and re-layouts: 1.45 us -> 0.19 us  [unstacked(): both[:, low:low + C].reshape(3, 3, C, C).transpose(3, 2, 0, 1)]
where the time goes in v3:
time: 104 us
  Pallas kernels  88.9 us (85%)
  local copies, waits for them, and re-layouts  12.9 us (12%)
  other arithmetic  1.63 us (2%)
    pallas_call x1, Pallas kernels, whole(): pl.pallas_call(functools.partial(whole_kernel, flat, row_count, col_count...  88.9 us
    unnamed x21, local copies, waits for them, and re-layouts  7.96 us
    reshape x4, local copies, waits for them, and re-layouts, unstacked(): both[:, low:low + C].reshape(3, 3, C, C).transpose(3, 2, 0, 1)  3.26 us

profile of v3, /device:TPU:0, one launch (start us, length us, event | category | flops | bytes accessed | tf_op | source)
XLA Modules:
  0.0 104.1 jit_solution(17063769130972767309)
XLA Ops:
  0.6 1.5 %copy.34 = bf16[48,8,128]{2,0,1:T(8,128)(2,1)} copy(bf16[48,8,128]{2,1,0:T(8,128)(2,1)} %param.12) | data formatting | bytes 196608 | tf_op args[2]
  2.2 1.1 %copy.19 = f32[3,3,48,48]{3,2,1,0:T(8,128)S(1)} copy(f32[3,3,48,48]{2,3,1,0:T(8,128)} %bitcast.39) | data formatting | bytes 165888 | tf_op jit(solution)/shard_map/transpose | solution.py:499
  3.3 0.0 copy-done.4
  3.3 0.1 copy.20
  3.4 0.0 copy-start.5
  3.4 0.8 select_maximum_fusion.1.refs_3_
  4.2 0.1 copy-done.5
  4.4 0.1 copy.21
  4.5 0.8 copy-done.6
  5.3 0.1 copy.22
  5.4 0.0 copy-start.2
  5.4 0.8 select_maximum_fusion.refs_4_
  6.3 0.0 copy-done.3
  6.3 0.9 copy.33
  7.2 1.3 %copy.32 = f32[48,16,256]{2,0,1:T(8,128)} copy(f32[48,16,256]{2,1,0:T(8,128)S(1)} %copy-done.2) | data formatting | bytes 1572864 | tf_op args[1]
  8.5 88.9 %shard_map.145 = (f32[16,48,256]{2,1,0:T(8,128)}, bf16[8,48,128]{2,1,0:T(8,128)(2,1)}, f32[432,128]{1,0:T(8,128)}, f32[432,128]{1,0:T(8,128)}) custom-call(bf16[16,48,256]{2,1,0:T(8,128)(2,1)} %bitcast.28, f32[16,48,256]{2,1,0:T(8,128)} %bitcast.27, bf16[8,48,128]{2,1,0:T(8,128)(2,1)} %bitcast.38, f32[432,128]{1,0:T(8,128)} %select_maximum_fusion.1.refs_3_, ...), custom_call_target="tpu_custom_call" | custom-call | tf_op jit(solution)/shard_map/pallas_call | solution.py:485
  97.5 2.5 %copy.27 = f32[48,16,256]{2,1,0:T(8,128)} copy(f32[48,16,256]{2,0,1:T(8,128)} %bitcast.37) | data formatting | bytes 1572864
  100.0 0.0 copy-done.7
  100.0 0.7 copy.28
  100.7 0.2 fusion
  100.9 0.8 copy.26
  101.7 0.8 copy.25
  102.5 0.8 copy.23
  103.3 0.8 copy.24
  (9 shorter events, 0.0 us)
Async XLA Ops:
  2.2 1.1 %copy-start.4 = (f32[48,48,3,3]{1,0,3,2:T(8,128)S(1)}, f32[48,48,3,3]{1,0,3,2:T(8,128)}, u32[]{:S(2)}) copy-start(f32[48,48,3,3]{1,0,3,2:T(8,128)} %param.14) | copy-start | bytes 248836
  3.4 0.9 copy-start.5
  4.4 0.9 copy-start.6
  5.3 1.0 copy-start.3
  5.4 1.8 %copy-start.2 = (f32[48,16,256]{2,1,0:T(8,128)S(1)}, f32[48,16,256]{2,1,0:T(8,128)}, u32[]{:S(2)}) copy-start(f32[48,16,256]{2,1,0:T(8,128)} %param.11) | copy-start | bytes 2359300
  97.4 2.6 %copy-start.7 = (bf16[8,48,128]{2,1,0:T(8,128)(2,1)S(1)}, bf16[8,48,128]{2,1,0:T(8,128)(2,1)}, u32[]{:S(2)}) copy-start(bf16[8,48,128]{2,1,0:T(8,128)(2,1)} %get-tuple-element.11) | copy-start | bytes 294916
  97.4 3.2 %copy-start = (f32[432,128]{1,0:T(8,128)S(1)}, f32[432,128]{1,0:T(8,128)}, u32[]{:S(2)}) copy-start(f32[432,128]{1,0:T(8,128)} %get-tuple-element.12) | copy-start | bytes 663556
  97.5 3.2 %copy-start.1 = (f32[432,128]{1,0:T(8,128)S(1)}, f32[432,128]{1,0:T(8,128)}, u32[]{:S(2)}) copy-start(f32[432,128]{1,0:T(8,128)} %get-tuple-element.13) | copy-start | bytes 663556

commit v4 on v3

--- a/solution.py
+++ b/solution.py
@@ -336,7 +336,7 @@
         gathered = chosen(lambda j: beside[k, j, 0 : 4 * C], 4 * C)
         for p in range(4):
             extend(own[k, p], gathered[p * C : (p + 1) * C, :], above[k, p], below[k, p])
-            full = ext[...]
+            full = ext[...].astype(BF16)
             for i, (a, b) in enumerate(taps):
                 moved = rolled(full, (a - 1) * T + (b - 1))
                 attacked_cols[p, i * C : (i + 1) * C, :] = moved.astype(BF16)
@@ -347,17 +347,17 @@
         for i, (a, b) in enumerate(taps):
             py, dy = [(1, -1), (0, 0), (1, 0)][a]
             px, dx = [(1, -1), (0, 0), (1, 0)][b]
-            moved = rolled(hidden[2 * py + px], dy * T + dx)
-            hidden_cols[i * C : (i + 1) * C, :] = moved.astype(BF16)
+            moved = rolled(hidden[2 * py + px].astype(BF16), dy * T + dx)
+            hidden_cols[i * C : (i + 1) * C, :] = moved
         predict = dot(ahead_two, hidden_cols[...])
         ext[...] = predict
-        residual = (predict - target[...]) * inside
+        residual = ((predict - target[...]) * inside).astype(BF16)
         wide[0:C, :] = jnp.zeros((C, high - low), BF16)
-        wide[SECOND : SECOND + C, :] = (residual * owned)[:, low:high].astype(BF16)
+        wide[SECOND : SECOND + C, :] = (residual[:, low:high].astype(F32) * owned[:, low:high]).astype(BF16)
         total = dot_nt(hidden_cols[:, low:high], wide[...])
         wide[SECOND : SECOND + C, :] = jnp.zeros((C, high - low), BF16)
         for i, shift in enumerate((0, 1, T, T + 1)):
-            rest_cols[i * C : (i + 1) * C, :] = rolled(residual, shift).astype(BF16)
+            rest_cols[i * C : (i + 1) * C, :] = rolled(residual, shift)
         hidden_grad = dot(spread_weight[...], rest_cols[...])
         for p in range(4):
             pre_grad = hidden_grad[p * C : (p + 1) * C, :] * slope[p]
@@ -371,10 +371,10 @@
             copy.start()
 
         def input_side(p):
-            pre_grad = hidden[p]
+            pre_grad = hidden[p].astype(BF16)
             for i, (a, b) in enumerate(taps):
                 moved = rolled(pre_grad, -((a - 1) * T + (b - 1)))
-                pre_cols[i * C : (i + 1) * C, :] = moved[:, low:high].astype(BF16)
+                pre_cols[i * C : (i + 1) * C, :] = moved[:, low:high]
             input_grad = dot(back_one, pre_cols[...])
             moved = jnp.clip(
                 perturb[p, :, low:high] + step_size * jnp.tanh(input_grad), -clip_bound, clip_bound

time: 104 us -> 103 us (level)
  Pallas kernels: 88.9 us -> 87.6 us
    pallas_call x1, Pallas kernels: 88.9 us -> 87.6 us  [whole(): pl.pallas_call(functools.partial(whole_kernel, flat, row_count, col_count...]
where the time goes in v4:
time: 103 us
  Pallas kernels  87.6 us (85%)
  local copies, waits for them, and re-layouts  12.9 us (13%)
  other arithmetic  1.63 us (2%)
    pallas_call x1, Pallas kernels, whole(): pl.pallas_call(functools.partial(whole_kernel, flat, row_count, col_count...  87.6 us
    unnamed x21, local copies, waits for them, and re-layouts  7.96 us
    reshape x4, local copies, waits for them, and re-layouts, unstacked(): both[:, low:low + C].reshape(3, 3, C, C).transpose(3, 2, 0, 1)  3.26 us

profile of v4, /device:TPU:0, one launch (start us, length us, event | category | flops | bytes accessed | tf_op | source)
XLA Modules:
  0.0 102.8 jit_solution(9740853874251044997)
XLA Ops:
  0.6 1.5 %copy.34 = bf16[48,8,128]{2,0,1:T(8,128)(2,1)} copy(bf16[48,8,128]{2,1,0:T(8,128)(2,1)} %param.12) | data formatting | bytes 196608 | tf_op args[2]
  2.2 1.1 %copy.19 = f32[3,3,48,48]{3,2,1,0:T(8,128)S(1)} copy(f32[3,3,48,48]{2,3,1,0:T(8,128)} %bitcast.39) | data formatting | bytes 165888 | tf_op jit(solution)/shard_map/transpose | solution.py:499
  3.3 0.1 copy.20
  3.4 0.0 copy-start.5
  3.4 0.8 select_maximum_fusion.1.refs_3_
  4.2 0.1 copy-done.5
  4.4 0.1 copy.21
  4.5 0.8 copy-done.6
  5.3 0.1 copy.22
  5.4 0.0 copy-start.2
  5.4 0.8 select_maximum_fusion.refs_4_
  6.3 0.0 copy-done.3
  6.3 0.9 copy.33
  7.2 0.0 copy-done.2
  7.2 1.3 %copy.32 = f32[48,16,256]{2,0,1:T(8,128)} copy(f32[48,16,256]{2,1,0:T(8,128)S(1)} %copy-done.2) | data formatting | bytes 1572864 | tf_op args[1]
  8.5 87.6 %shard_map.145 = (f32[16,48,256]{2,1,0:T(8,128)}, bf16[8,48,128]{2,1,0:T(8,128)(2,1)}, f32[432,128]{1,0:T(8,128)}, f32[432,128]{1,0:T(8,128)}) custom-call(bf16[16,48,256]{2,1,0:T(8,128)(2,1)} %bitcast.28, f32[16,48,256]{2,1,0:T(8,128)} %bitcast.27, bf16[8,48,128]{2,1,0:T(8,128)(2,1)} %bitcast.38, f32[432,128]{1,0:T(8,128)} %select_maximum_fusion.1.refs_3_, ...), custom_call_target="tpu_custom_call" | custom-call | tf_op jit(solution)/shard_map/pallas_call | solution.py:485
  96.2 0.0 copy-start.7
  96.2 2.5 %copy.27 = f32[48,16,256]{2,1,0:T(8,128)} copy(f32[48,16,256]{2,0,1:T(8,128)} %bitcast.37) | data formatting | bytes 1572864
  98.7 0.7 copy.28
  99.4 0.2 fusion
  99.6 0.8 copy.26
  100.4 0.8 copy.25
  101.2 0.8 copy.23
  102.0 0.8 copy.24
  (9 shorter events, 0.0 us)
Async XLA Ops:
  2.2 1.1 %copy-start.4 = (f32[48,48,3,3]{1,0,3,2:T(8,128)S(1)}, f32[48,48,3,3]{1,0,3,2:T(8,128)}, u32[]{:S(2)}) copy-start(f32[48,48,3,3]{1,0,3,2:T(8,128)} %param.14) | copy-start | bytes 248836
  3.4 0.9 copy-start.5
  4.4 0.9 copy-start.6
  5.3 1.0 copy-start.3
  5.4 1.8 %copy-start.2 = (f32[48,16,256]{2,1,0:T(8,128)S(1)}, f32[48,16,256]{2,1,0:T(8,128)}, u32[]{:S(2)}) copy-start(f32[48,16,256]{2,1,0:T(8,128)} %param.11) | copy-start | bytes 2359300
  96.2 2.6 %copy-start.7 = (bf16[8,48,128]{2,1,0:T(8,128)(2,1)S(1)}, bf16[8,48,128]{2,1,0:T(8,128)(2,1)}, u32[]{:S(2)}) copy-start(bf16[8,48,128]{2,1,0:T(8,128)(2,1)} %get-tuple-element.11) | copy-start | bytes 294916
  96.2 3.2 %copy-start = (f32[432,128]{1,0:T(8,128)S(1)}, f32[432,128]{1,0:T(8,128)}, u32[]{:S(2)}) copy-start(f32[432,128]{1,0:T(8,128)} %get-tuple-element.12) | copy-start | bytes 663556
  96.2 3.2 %copy-start.1 = (f32[432,128]{1,0:T(8,128)S(1)}, f32[432,128]{1,0:T(8,128)}, u32[]{:S(2)}) copy-start(f32[432,128]{1,0:T(8,128)} %get-tuple-element.13) | copy-start | bytes 663556
